TPU v7x, 256 devices: a whole 4x4x8 slice. The times are simulated.
256 devices in a mesh: ctx: 8 (over x, y_hi), mp: 32 (over z, y_lo, core).
Axes of the slice: x: 4, y: 4 (y_hi: 2, y_lo: 2; y = y_hi * 2 + y_lo), z: 8, core: 2. Of those that a mesh axis runs over, the one named last changes fastest.
Arguments:
- activations: bfloat16 [8192, 4096], P('ctx', 'mp'), may hold values from -36 to 36
- norm_gain: float32 [4096], P('mp'), may hold values from 0.1 to 1.9
- w_in: bfloat16 [4096, 3, 4096], P('ctx', None, 'mp'), may hold values from -0.09375 to 0.09375
- tail_rows: bfloat16 [3, 4096, 2], P(None, 'mp'), may hold values from -4 to 4
- short_filter: float32 [3, 3, 4096], P(None, None, 'mp'), may hold values from -3 to 3
- decay_rate: float32 [4096, 16], P('mp'), may hold values from 2.4414063e-05 to 0.08, as said below
- residue: float32 [4096, 16], P('mp'), may hold values from -1.5 to 1.5
- skip_gain: float32 [4096], P('mp'), may hold values from -4 to 4
- state_in: float32 [4096, 16], P('mp'), may hold values from -4 to 4
- w_out: bfloat16 [4096, 4096], P('mp', 'ctx'), may hold values from -0.1875 to 0.1875
Outputs:
- block_out: bfloat16 [8192, 4096], P('ctx', 'mp')
- state_out: float32 [4096, 16], P('mp')
Inputs may be any that keep to these rules, and one draw needn't show every extreme that they name: `decay_rate`: every rate lies between 0.2/8192 and 0.08; any share of the modes may be slow (below 2/8192) or fast.
All inputs are finite; a program needn't handle non-finite values.
Results may differ from a plain program's by a relative error of at most 0.03.
Values may be sent and summed in bfloat16 or wider, within the bound.
A program may use at most 64 MiB of HBM per device.

v0:
```python
import math

import jax
import jax.numpy as jnp
import numpy as np
from jax import lax
from jax.sharding import PartitionSpec as P

highest = lax.Precision.HIGHEST


def from_behind(block, axis, distance):
    devices = range(lax.axis_size(axis))
    route = [(i - distance, i) for i in devices if i - distance in devices]
    return lax.ppermute(block, axis, route)


def pick_rows(array_in, offset, share):
    return lax.dynamic_slice_in_dim(array_in, offset, share, 0)


def chain_step(first, second):
    return (first[0] * second[0], second[0] * first[1] + second[1])


def block_powers(rate_rows, block_size):
    steps_in = jnp.arange(block_size, dtype=jnp.float32)
    return jnp.exp(-rate_rows[:, :, None] * steps_in[None, None, :])


def carried_response(entering, rate_rows, residues, block_size):
    powers = block_powers(rate_rows, block_size)
    lifted = residues[:, :, None] * jnp.exp(-rate_rows)[:, :, None] * powers
    return jnp.einsum("ckn,cnt->ckt", entering, lifted, precision=highest)


def initial_response(initial, rate_rows, residues, length):
    block_size = math.gcd(64, length)
    blocks = length // block_size
    index_k = jnp.arange(blocks, dtype=jnp.float32) * block_size
    carried = jnp.exp(-rate_rows[:, None, :] * index_k[None, :, None]) * initial[:, None, :]
    return carried_response(carried, rate_rows, residues, block_size).reshape(
        initial.shape[0], length
    )


def modal_conv(signal, rate_rows, residues, skip_rows, initial):
    channels, length = signal.shape
    block_size = math.gcd(64, length)
    blocks = length // block_size
    values = signal.astype(jnp.float32)
    shaped = values.reshape(channels, blocks, block_size)
    powers = block_powers(rate_rows, block_size)
    scales = jnp.sqrt(-jnp.expm1(-2.0 * rate_rows))
    kernel = jnp.einsum("cn,cnb->cb", residues * scales, powers, precision=highest)
    offsets = np.arange(block_size)[:, None] - np.arange(block_size)[None, :]
    clipped = np.clip(offsets, 0, block_size - 1)
    toeplitz = jnp.where(offsets[None] >= 0, kernel[:, clipped], 0.0)
    within = jnp.einsum("cts,cks->ckt", toeplitz, shaped, precision=highest)
    loading = jnp.einsum(
        "cks,cns->ckn", shaped, scales[:, :, None] * powers[:, :, ::-1], precision=highest
    )
    decays = jnp.broadcast_to(jnp.exp(-rate_rows * block_size)[:, None, :], loading.shape)
    decay_all, block_ends = lax.associative_scan(chain_step, (decays, loading), axis=1)
    entering = jnp.concatenate([jnp.zeros_like(block_ends[:, :1]), block_ends[:, :-1]], axis=1)
    response = (within + carried_response(entering, rate_rows, residues, block_size)).reshape(
        channels, length
    )
    response = response + initial_response(initial, rate_rows, residues, length)
    final = block_ends[:, -1] + jnp.exp(-rate_rows * length) * initial
    return (response + skip_rows[:, None] * values, final)


def local(
    activations,
    norm_gain,
    w_in,
    tail_rows,
    short_filter,
    decay_rate,
    residue,
    skip_gain,
    state_in,
    w_out,
):
    tok_rows, feature_width = activations.shape
    model_width = feature_width * lax.axis_size("mp")
    act_float = activations.astype(jnp.float32)
    squares = lax.psum(jnp.sum(act_float * act_float, axis=1), "mp")
    inverse = lax.rsqrt(squares / model_width + 1e-06)
    normed = (act_float * inverse[:, None] * norm_gain[None, :]).astype(jnp.bfloat16)
    panel = lax.all_gather(w_in, "ctx", axis=0, tiled=True).reshape(model_width, 3 * feature_width)
    proj_sum = lax.dot_general(
        panel,
        lax.all_gather(normed, "mp", axis=1, tiled=True),
        (((0,), (1,)), ((), ())),
        preferred_element_type=jnp.float32,
    )
    projected = proj_sum.astype(jnp.bfloat16).reshape(3, feature_width, tok_rows)
    incoming = from_behind(projected[:, :, -2:], "ctx", 1)
    incoming = jnp.where(lax.axis_index("ctx") == 0, tail_rows, incoming)
    extended = jnp.concatenate([incoming, projected], axis=2).astype(jnp.float32)
    smoothed = short_filter[0][:, :, None] * extended[:, :, 2:]
    smoothed = smoothed + short_filter[1][:, :, None] * extended[:, :, 1:-1]
    smoothed = smoothed + short_filter[2][:, :, None] * extended[:, :, :-2]
    query = smoothed[0]
    mixed = (smoothed[1] * smoothed[2]).astype(jnp.bfloat16)
    share = feature_width // lax.axis_size("ctx")
    offset = lax.axis_index("ctx") * share
    whole = lax.all_to_all(mixed, "ctx", split_axis=0, concat_axis=1, tiled=True)
    filtered, final_part = modal_conv(
        whole,
        pick_rows(decay_rate, offset, share),
        pick_rows(residue, offset, share),
        pick_rows(skip_gain, offset, share),
        pick_rows(state_in, offset, share),
    )
    response = lax.all_to_all(filtered, "ctx", split_axis=1, concat_axis=0, tiled=True)
    final_state = lax.all_gather(final_part, "ctx", axis=0, tiled=True)
    gated = (query * response).astype(jnp.bfloat16)
    out_panel = lax.all_gather(w_out, "ctx", axis=1, tiled=True)
    branch = (
        lax.psum_scatter(
            lax.dot_general(
                out_panel, gated, (((0,), (0,)), ((), ())), preferred_element_type=jnp.float32
            ).astype(jnp.bfloat16),
            "mp",
            scatter_dimension=0,
            tiled=True,
        )
        .astype(jnp.float32)
        .T
    )
    return ((act_float + branch).astype(jnp.bfloat16), final_state)


def solution(mesh):
    placed = (
        P("ctx", "mp"),
        P("mp"),
        P("ctx", None, "mp"),
        P(None, "mp", None),
        P(None, None, "mp"),
        P("mp", None),
        P("mp", None),
        P("mp"),
        P("mp", None),
        P("mp", "ctx"),
    )
    return jax.shard_map(
        local,
        mesh=mesh,
        in_specs=placed,
        out_specs=(P("ctx", "mp"), P("mp", None)),
        check_vma=False,
    )
```

profile of v0, /device:TPU:1, one launch (start us, length us, event | category | flops | bytes accessed | tf_op | source)
XLA Modules:
  0.0 456.1 jit_solution(16043692956074559367)
XLA Ops:
  7.3 1.9 copy.85
  10.4 57.5 %psum.7 = f32[1024]{0:T(1024)S(1)} all-reduce(f32[1024]{0:T(1024)S(1)} %fusion.2), channel_id=1, replica_groups=mesh['ctx'=8,'mp'=32] {'mp'}, use_global_device_ids=true, to_apply=%region_1.0 | all-reduce | flops 1024 | bytes 8192 | tf_op jit(solution)/shard_map/psum | solution.py:89
  67.9 1.9 fusion.4
  71.5 15.3 %all-gather.6.cloned.1.call-done = bf16[4096,3,128]{0,2,1:T(8,128)(2,1)} async-done(((bf16[512,3,128]{0,2,1:T(8,128)(2,1)}), bf16[4096,3,128]{0,2,1:T(8,128)(2,1)}) %all-gather.6.cloned.1.call-update) | async-done | bytes 3145744 | tf_op jit(solution)/shard_map/all_gather | solution.py:92
  86.8 92.1 %all-gather.4.cloned.1.call-done = bf16[1024,4096]{1,0:T(8,128)(2,1)} async-done(((bf16[1024,128]{1,0:T(8,128)(2,1)}), bf16[1024,4096]{1,0:T(8,128)(2,1)}) %all-gather.4.cloned.1.call-update) | async-done | bytes 8388624 | tf_op jit(solution)/shard_map/all_gather | solution.py:95
  178.9 7.7 %convolution_convert_fusion = bf16[1024,384]{0,1:T(8,128)(2,1)S(1)} fusion(bf16[1024,4096]{1,0:T(8,128)(2,1)} %all-gather.4.cloned.1.call-done, bf16[4096,384]{0,1:T(8,128)(2,1)} %bitcast.65), kind=kOutput, calls=%fused_computation.7 | convolution fusion | flops 3221618688 | bytes 12320768 | tf_op jit(solution)/shard_map/dot_general | solution.py:93
  186.8 3.6 collective-permute-start
  190.7 1.8 collective-permute-done
  194.8 7.3 %all-to-all-start = ((bf16[8,16,1024]{2,1,0:T(8,128)(2,1)}), bf16[8,16,1024]{2,1,0:T(8,128)(2,1)S(1)}, u32[]{:S(2)}, u32[]{:S(2)}) async-start(bf16[8,16,1024]{2,1,0:T(8,128)(2,1)} %bitcast.7), calls=%async_computation | async-start | bytes 524288 | tf_op jit(solution)/shard_map/all_to_all | solution.py:110
  205.9 3.5 all-to-all-done
  210.9 2.9 slice.235
  213.9 2.3 slice.195
  216.2 2.3 slice.194
  218.6 1.9 slice.233
  223.1 1.3 slice.231
  235.0 6.2 %pad.47 = f32[16,4,16]{1,2,0:T(8,128)S(1)} pad(f32[16,2,16]{1,2,0:T(8,128)} %pad_add_fusion, f32[]{:T(128)} %constant.7.clone.1), padding=0_0_0x1_0_1x0_0_0 | pad | bytes 6148 | tf_op jit(solution)/shard_map/pad | solution.py:64
  247.3 1.3 pad.50
  248.6 1.4 pad.51
  251.0 1.6 pad.52
  252.6 1.6 pad.53
  255.2 2.1 pad.54
  257.3 2.2 pad.55
  259.5 3.2 pad.95
  262.7 3.2 pad.57
  266.2 3.2 pad.56
  270.1 14.2 %gather_fusion = f32[4096,16]{1,0:T(8,128)} fusion(f32[16,64]{0,1:T(8,128)S(1)} %bitcast.53, s32[4096]{0:T(1024)S(1)} %copy-done.5), kind=kCustom, calls=%fused_computation | custom fusion | bytes 540672 | tf_op jit(solution)/shard_map/gather | solution.py:58
  284.3 2.3 copy.90
  291.1 11.4 %all_to_all.29 = f32[16,8,1024]{2,0,1:T(8,128)S(1)} all-to-all(f32[16,8,1024]{2,0,1:T(8,128)S(1)} %copy_add_fusion), channel_id=1, replica_groups=mesh['ctx'=8,'mp'=32] {'ctx'}, dimensions={1} | all-to-all | bytes 1048576 | tf_op jit(solution)/shard_map/all_to_all | solution.py:118
  302.6 6.9 %convert_bitcast_fusion = bf16[4096,1024]{0,1:T(8,128)(2,1)} fusion(bf16[128,1024]{1,0:T(8,128)(2,1)S(1)} %fusion.8, bf16[128,4096]{1,0:T(8,128)(2,1)} %all-gather.8.cloned.1.call-done), kind=kOutput, calls=%fused_computation.1 | convolution fusion | flops 1077936128 | bytes 9699328 | tf_op jit(solution)/shard_map/dot_general | solution.py:124
  309.5 11.9 %copy.103 = bf16[4096,1024]{1,0:T(8,128)(2,1)} copy(bf16[4096,1024]{0,1:T(8,128)(2,1)} %convert_bitcast_fusion) | data formatting | bytes 16777216
  321.4 28.2 %all_gather.15 = f32[128,16]{1,0:T(8,128)S(1)} all-gather(f32[16,16]{1,0:T(8,128)S(1)} %get-tuple-element.20), channel_id=1, replica_groups=mesh['ctx'=8,'mp'=32] {'ctx'}, dimensions={0}, use_global_device_ids=true | all-gather | bytes 9216 | tf_op jit(solution)/shard_map/all_gather | solution.py:119
  350.3 97.4 %reduce-scatter.4.cloned.1.call-done = bf16[128,1024]{1,0:T(8,128)(2,1)} async-done(((bf16[4096,1024]{1,0:T(8,128)(2,1)}), bf16[128,1024]{1,0:T(8,128)(2,1)}) %reduce-scatter.4.cloned.1.call-update) | async-done | bytes 262160
  (135 shorter events, 39.8 us)
Async XLA Ops:
  7.2 183.3 %copy-start = (f32[128,16]{0,1:T(8,128)S(1)}, f32[128,16]{0,1:T(8,128)}, u32[]{:S(2)}) copy-start(f32[128,16]{0,1:T(8,128)} %param.19) | copy-start | bytes 24580
  7.2 63.4 %copy-start.18 = (f32[3,3,128]{2,1,0:T(4,128)S(1)}, f32[3,3,128]{2,1,0:T(4,128)}, u32[]{:S(2)}) copy-start(f32[3,3,128]{2,1,0:T(4,128)} %param.17) | copy-start | bytes 13828
  7.2 63.4 %copy-start.16 = (f32[128,16]{0,1:T(8,128)S(1)}, f32[128,16]{0,1:T(8,128)}, u32[]{:S(2)}) copy-start(f32[128,16]{0,1:T(8,128)} %param.21) | copy-start | bytes 24580
  7.2 63.4 %copy-start.17 = (f32[128,16]{0,1:T(8,128)S(1)}, f32[128,16]{0,1:T(8,128)}, u32[]{:S(2)}) copy-start(f32[128,16]{0,1:T(8,128)} %param.18) | copy-start | bytes 24580
  7.2 79.6 %all-gather.6.cloned.1.call-start = ((), (), s32[]{:S(2)}) async-start(), calls=%async_computation.4 | async-start | bytes 3538944 | tf_op jit(solution)/shard_map/all_gather | solution.py:92
  9.2 169.7 %all-gather.4.cloned.1.call-start = ((), (), s32[]{:S(2)}) async-start(), calls=%async_computation.3 | async-start | bytes 8650752 | tf_op jit(solution)/shard_map/all_gather | solution.py:95
  69.8 232.8 %all-gather.8.cloned.1.call-start = ((), (), s32[]{:S(2)}) async-start(), calls=%async_computation.5 | async-start | bytes 1179648 | tf_op jit(solution)/shard_map/all_gather | solution.py:121
  70.8 115.9 %copy-start.11 = (f32[16,16]{1,0:T(8,128)}, f32[16,16]{1,0:T(8,128)S(1)}, u32[]{:S(2)}) copy-start(f32[16,16]{1,0:T(8,128)S(1)} %copy.106) | copy-start | bytes 3076
  71.4 147.1 %copy-start.7 = (f32[16,16]{1,0:T(8,128)}, f32[16,16]{1,0:T(8,128)S(1)}, u32[]{:S(2)}) copy-start(f32[16,16]{1,0:T(8,128)S(1)} %get-tuple-element.27) | copy-start | bytes 3076
  71.4 151.6 %copy-start.9 = (f32[16,16]{1,0:T(8,128)}, f32[16,16]{1,0:T(8,128)S(1)}, u32[]{:S(2)}) copy-start(f32[16,16]{1,0:T(8,128)S(1)} %get-tuple-element.28) | copy-start | bytes 3076
  71.4 154.5 %copy-start.10 = (f32[16,16]{1,0:T(8,128)}, f32[16,16]{1,0:T(8,128)S(1)}, u32[]{:S(2)}) copy-start(f32[16,16]{1,0:T(8,128)S(1)} %get-tuple-element.22) | copy-start | bytes 3076
  178.9 11.6 %copy-start.19 = (bf16[3,128,2]{1,2,0:T(2,128)(2,1)S(1)}, bf16[3,128,2]{1,2,0:T(2,128)(2,1)}, u32[]{:S(2)}) copy-start(bf16[3,128,2]{1,2,0:T(2,128)(2,1)} %param.16) | copy-start | bytes 4612
  186.8 5.7 %collective-permute-start = (bf16[3,128,2]{2,1,0:T(8,128)(2,1)S(1)}, bf16[3,128,2]{2,1,0:T(8,128)(2,1)S(1)}, u32[]{:S(2)}, u32[]{:S(2)}) collective-permute-start(bf16[3,128,2]{2,1,0:T(8,128)(2,1)S(1)} %slice.240), channel_id=1, source_target_pairs={{0,32},{32,64},{64,96},{96,128},{128,160},{160,192},{192,224},{1,3... | collective-permute-start | bytes 4616 | tf_op jit(solution)/shard_map/ppermute | solution.py:15
  194.0 8.9 %copy-start.22 = (f32[128]{0:T(128)S(1)}, f32[128]{0:T(128)}, u32[]{:S(2)}) copy-start(f32[128]{0:T(128)} %param.20) | copy-start | bytes 1540
  194.1 11.3 %copy-start.14 = (s32[4096]{0:T(1024)S(1)}, s32[4096]{0:T(1024)}, u32[]{:S(2)}) copy-start(s32[4096]{0:T(1024)} %constant.70) | copy-start | bytes 49156
  194.8 14.6 %all-to-all-start = ((bf16[8,16,1024]{2,1,0:T(8,128)(2,1)}), bf16[8,16,1024]{2,1,0:T(8,128)(2,1)S(1)}, u32[]{:S(2)}, u32[]{:S(2)}) async-start(bf16[8,16,1024]{2,1,0:T(8,128)(2,1)} %bitcast.7), calls=%async_computation | async-start | bytes 524288 | tf_op jit(solution)/shard_map/all_to_all | solution.py:110
  202.2 245.5 %reduce-scatter.4.cloned.1.call-start = ((), (), s32[]{:S(2)}) async-start(), calls=%async_computation.6 | async-start | bytes 8650752
  242.5 7.5 %copy-start.4 = (f32[16,15,16]{1,2,0:T(8,128)S(1)}, f32[16,15,16]{1,2,0:T(8,128)}, u32[]{:S(2)}) copy-start(f32[16,15,16]{1,2,0:T(8,128)} %slice.231) | copy-start | bytes 46084
  246.1 8.1 %copy-start.3 = (f32[16,31,16]{1,2,0:T(8,128)S(1)}, f32[16,31,16]{1,2,0:T(8,128)}, u32[]{:S(2)}) copy-start(f32[16,31,16]{1,2,0:T(8,128)} %slice.233) | copy-start | bytes 95236
  250.9 15.1 %copy-start.2 = (f32[16,63,16]{1,2,0:T(8,128)S(1)}, f32[16,63,16]{1,2,0:T(8,128)}, u32[]{:S(2)}) copy-start(f32[16,63,16]{1,2,0:T(8,128)} %slice.235) | copy-start | bytes 193540
  250.9 15.1 %copy-start.8 = (f32[16,16]{1,0:T(8,128)S(1)}, f32[16,16]{1,0:T(8,128)}, u32[]{:S(2)}) copy-start(f32[16,16]{1,0:T(8,128)} %copy-done.7) | copy-start | bytes 3076
  255.0 14.6 %copy-start.6 = (f32[16,16]{1,0:T(8,128)S(1)}, f32[16,16]{1,0:T(8,128)}, u32[]{:S(2)}) copy-start(f32[16,16]{1,0:T(8,128)} %copy.107) | copy-start | bytes 3076
  255.0 14.6 %copy-start.12 = (f32[16,16]{1,0:T(8,128)S(1)}, f32[16,16]{1,0:T(8,128)}, u32[]{:S(2)}) copy-start(f32[16,16]{1,0:T(8,128)} %copy-done.11) | copy-start | bytes 3076
  255.1 14.6 %copy-start.13 = (f32[16,16]{1,0:T(8,128)S(1)}, f32[16,16]{1,0:T(8,128)}, u32[]{:S(2)}) copy-start(f32[16,16]{1,0:T(8,128)} %copy.105) | copy-start | bytes 3076
  255.2 14.9 %copy-start.5 = (s32[4096]{0:T(1024)S(1)}, s32[4096]{0:T(1024)}, u32[]{:S(2)}) copy-start(s32[4096]{0:T(1024)} %broadcast_clamp_fusion) | copy-start | bytes 49156
  284.3 2.3 copy-start.15
  286.6 2.3 copy-start.21
  290.1 0.7 copy-start.20
  321.4 127.5 %copy-start.1 = (bf16[1024,128]{1,0:T(8,128)(2,1)S(1)}, bf16[1024,128]{1,0:T(8,128)(2,1)}, u32[]{:S(2)}) copy-start(bf16[1024,128]{1,0:T(8,128)(2,1)} %param.13) | copy-start | bytes 786436
Sparse Core Ops, SparseCore 0:
  10.5 76.2 all-gather.5
  89.1 89.7 all-gather.3
  181.4 49.5 all-gather.7
  321.5 126.1 reduce-scatter.3
where the time goes:
time: 459 us; the launch traced here: 456 us
  waiting for transfers between devices  211 us (46%)
  blocking collectives  97.1 us (21%)
  local copies, waits for them, and re-layouts  85.8 us (19%)
  matrix products  19.3 us (4%)
  other arithmetic  17.2 us (4%)
  between operations  14.5 us (3%)
  starting transfers between devices  11.3 us (2%)
    unnamed x5, waiting for transfers between devices  98.1 us
    all_gather x1, waiting for transfers between devices, local(): lax.all_gather(normed, 'mp', axis=1, tiled=True)  92.1 us
    psum x1, blocking collectives, local(): squares = lax.psum(jnp.sum(act_float * act_float, axis=1), 'mp')  57.5 us
    all_gather x1, blocking collectives, local(): final_state = lax.all_gather(final_part, 'ctx', axis=0, tiled=True)  28.2 us
    pad x12, local copies, waits for them, and re-layouts, modal_conv(): lax.associative_scan(chain_step, (decays, loading), axis=1)  26.4 us
    unnamed x55, local copies, waits for them, and re-layouts  20.5 us
    slice x19, local copies, waits for them, and re-layouts, modal_conv(): lax.associative_scan(chain_step, (decays, loading), axis=1)  20.2 us
    gather x2, local copies, waits for them, and re-layouts, modal_conv(): toeplitz = jnp.where(offsets[None] >= 0, kernel[:, clipped], 0.0)  16.5 us
  transfers between devices with their start and end apart: 6, of which 5 were waited for; matrix products, arithmetic and copies ran while one was open for 22% of the time, Pallas kernels for 0%

commit v1 on v0

v1 whole, which is shorter than its diff:
```python
import jax
import jax.numpy as jnp
from jax import lax
from jax.experimental import pallas as pl
from jax.experimental.pallas import tpu as pltpu
from jax.sharding import PartitionSpec as P

MESH = pl.DeviceIdType.MESH
F32, BF16 = jnp.float32, jnp.bfloat16

NI, NJ = 8, 32
NZ, NX = 8, 4
T, F, D, ORDER = 1024, 128, 4096, 16
H = T // 2
HG = H + 16
CH = 8
CL = T // CH
TILE = 256
N_SEND = 160
PLUS_HOPS = {"own0": 4, "own1": 3, "par1": 4}
MINUS_HOPS = {"own0": 3, "own1": 4, "par1": 3}


def one_minus_exp_neg(v):
    series = 1.0 - v * (1.0 / 8.0)
    for k in (7, 6, 5, 4, 3, 2):
        series = 1.0 - v * (1.0 / k) * series
    return v * series


def block_kernel(
    act, gain, w_local, tail, filt, rate, resid, skip, st_in, wout,
    out, st_out,
    xg, wg, ext, ssq, mx, ts, endb, ends, gf, gg, ws, wo, acc, osend, orecv,
    ssem, xr, wr, hr, er, wor, gr, orr,
):
    i, j = lax.axis_index("ctx"), lax.axis_index("mp")
    z, yl, c = j // 4, (j // 2) % 2, j % 2
    at = lambda zz, yy, cc: zz * 4 + yy * 2 + cc
    up, down = (z + 1) % NZ, (z + NZ - 1) % NZ
    dev_up, dev_down = (i, at(up, yl, c)), (i, at(down, yl, c))
    dev_y, dev_c = (i, at(z, 1 - yl, c)), (i, at(z, yl, 1 - c))
    ix_up, ix_down = (i + 2) % NI, (i + NI - 2) % NI
    pair = i + 1 - 2 * (i % 2)
    dev_xu, dev_xd, dev_yh = (ix_up, j), (ix_down, j), (pair, j)

    sends = []

    def send(src, dst, recv_sem, dev):
        copy = pltpu.make_async_remote_copy(
            src_ref=src, dst_ref=dst, send_sem=ssem.at[len(sends)], recv_sem=recv_sem,
            device_id=dev, device_id_type=MESH,
        )
        sends.append((copy, None))
        copy.start()

    def send_if(cond, src, dst, recv_sem, dev):
        copy = pltpu.make_async_remote_copy(
            src_ref=src, dst_ref=dst, send_sem=ssem.at[len(sends)], recv_sem=recv_sem,
            device_id=dev, device_id_type=MESH,
        )
        sends.append((copy, cond))
        pl.when(cond)(lambda: copy.start())

    def arrived(dst, recv_sem):
        pltpu.make_async_remote_copy(
            src_ref=dst, dst_ref=dst, send_sem=ssem.at[0], recv_sem=recv_sem,
            device_id=dev_up, device_id_type=MESH,
        ).wait_recv()

    barrier = pltpu.get_barrier_semaphore()

    def tell(dev):
        pl.semaphore_signal(barrier, inc=1, device_id=dev, device_id_type=MESH)

    for dev in (dev_up, dev_down, dev_y, dev_c):
        tell(dev)
    for k in range(1, NI):
        tell(((i + k) % NI, j))
    self_out = z == i
    for k in range(16):
        zz, cc = (z + k // 2) % NZ, (c + k % 2) % 2
        if k == 0:
            pl.when(jnp.logical_not(self_out))(lambda: tell((z, at(z, yl, c))))
        else:
            tell((z, at(zz, yl, cc)))

    g = gain[...]
    g_hi = g.astype(BF16)
    g_rest = g - g_hi.astype(F32)
    g_mid = g_rest.astype(BF16)
    g_lo = (g_rest - g_mid.astype(F32)).astype(BF16)
    row16 = lax.broadcasted_iota(jnp.int32, (16, F), 0)
    zero16 = jnp.zeros((16, F), F32)
    g_rows = jnp.where(
        row16 == 0, g_hi.astype(F32) + zero16,
        jnp.where(row16 == 1, g_mid.astype(F32) + zero16,
                  jnp.where(row16 == 2, g_lo.astype(F32) + zero16, zero16)),
    ).astype(BF16)
    for h in range(2):
        xg[h, j, 0:H, :] = act[h * H:(h + 1) * H, :]
        xg[h, j, H:HG, :] = g_rows
    wg[i, 0] = w_local[0:256, :]
    wg[i, 1] = w_local[256:512, :]
    for c2 in range(2):
        lo, hi = wout[:, c2 * F:(c2 + 1) * F], wout[:, (2 + c2) * F:(3 + c2) * F]
        ws[c2, 0] = jnp.where(yl == 0, lo, hi)
        ws[c2, 1] = jnp.where(yl == 0, hi, lo)

    peers = 4 + NI - 1 + 16
    pl.when(self_out)(lambda: pl.semaphore_wait(barrier, peers - 1))
    pl.when(jnp.logical_not(self_out))(lambda: pl.semaphore_wait(barrier, peers))

    def x_send(h, jj, dev):
        send(xg.at[h, jj], xg.at[h, jj], xr.at[h, jj], dev)

    def x_wait(h, jj):
        arrived(xg.at[h, jj], xr.at[h, jj])

    def w_send(ii, half, dev):
        send(wg.at[ii, half], wg.at[ii, half], wr.at[ii, half], dev)

    def w_wait(ii, half):
        arrived(wg.at[ii, half], wr.at[ii, half])

    for h in range(2):
        x_send(h, j, dev_y)
        x_send(h, j, dev_up)
        x_send(h, j, dev_down)
        x_send(h, j, dev_c)
    for half in range(2):
        w_send(i, half, dev_yh)
        w_send(i, half, dev_xu)
        w_send(i, half, dev_xd)

    def clear(r, carry):
        ext[:, pl.ds(8 + r * 128, 128), :] = jnp.zeros((3, 128, F), F32)
        ssq[pl.ds(r * 128, 128), :] = jnp.zeros((128, F), F32)
        return carry

    lax.fori_loop(0, T // 128, clear, 0)

    jp = at(z, 1 - yl, c)
    x_wait(1, jp)
    x_send(1, jp, dev_up)
    x_send(1, jp, dev_down)
    x_send(1, jp, dev_c)
    x_wait(0, jp)
    x_send(0, jp, dev_c)
    for half in range(2):
        w_wait(pair, half)
        w_send(pair, half, dev_xu)
        w_send(pair, half, dev_xd)

    def x_step(s):
        for plus in (True, False):
            zo = (z + NZ - s) % NZ if plus else (z + s) % NZ
            hops = PLUS_HOPS if plus else MINUS_HOPS
            dev = dev_up if plus else dev_down
            for name, h, yy in (("own0", 0, yl), ("own1", 1, yl), ("par1", 1, 1 - yl)):
                if s > hops[name]:
                    continue
                jj = at(zo, yy, c)
                x_wait(h, jj)
                if s < hops[name]:
                    x_send(h, jj, dev)
                if name == "own0":
                    x_send(h, jj, dev_y)
                x_send(h, jj, dev_c)

    def x_late(s):
        for zo in ((z + NZ - s) % NZ, (z + s) % NZ)[: 1 if s == NZ // 2 else 2]:
            jj = at(zo, 1 - yl, c)
            x_wait(0, jj)
            x_send(0, jj, dev_c)

    def x_other_core(s):
        for zo in ((z + NZ - s) % NZ, (z + s) % NZ)[: 1 if s in (0, NZ // 2) else 2]:
            for yy in range(2):
                for h in range(2):
                    x_wait(h, at(zo, yy, 1 - c))

    def multiply(zo, yy, r):
        h, rows = r // 2, pl.ds(pl.multiple_of((r % 2) * TILE, TILE), TILE)
        total = pl.ds(pl.multiple_of(r * TILE, TILE), TILE)
        parts, squares = [], None
        for cc in range(2):
            jj = at(zo, yy, cc)
            block = xg[h, jj, rows, :].astype(F32)
            gains = jnp.sum(xg[h, jj, pl.ds(H, 16), :].astype(F32), axis=0, keepdims=True)
            parts.append((block * gains).astype(BF16))
            squares = block * block if squares is None else squares + block * block
        ssq[total, :] += squares
        into = pl.ds(pl.multiple_of(8 + r * TILE, 8), TILE)
        product = jnp.dot(jnp.concatenate(parts, axis=1), wg[zo, yy], preferred_element_type=F32)
        for q in range(3):
            ext[q, into, :] += product[:, q * F:(q + 1) * F]

    def compute(s):
        blocks = 2 if s in (0, NZ // 2) else 4

        def body(k, carry):
            blk, r = k // 4, k % 4
            zo = (z + NZ - s + (blk // 2) * 2 * s) % NZ
            multiply(zo, blk % 2, r)
            return carry

        lax.fori_loop(0, blocks * 4, body, 0)

    x_step(1)
    for half in (0, 1):
        w_wait(ix_down, half)
        if half == 0:
            w_send(ix_down, 0, dev_xu)
        w_wait(ix_up, half)
        if half == 1:
            w_send(ix_up, 1, dev_xd)
    x_step(2)
    x_late(1)
    pd, pu = (pair + NI - 2) % NI, (pair + 2) % NI
    for half in (0, 1):
        w_wait(pd, half)
        if half == 0:
            w_send(pd, 0, dev_xu)
        w_wait(pu, half)
        if half == 1:
            w_send(pu, 1, dev_xd)
    x_step(3)
    x_late(2)
    far, pfar = (i + 4) % NI, (pair + 4) % NI
    for half in range(2):
        w_wait(far, half)
    for half in range(2):
        w_wait(pfar, half)
    x_other_core(0)
    compute(0)
    x_late(3)
    x_other_core(1)
    compute(1)
    x_step(4)

    slot = z * 2 + c
    for k in range(16):
        i2, c2 = (i + k // 2) % NI, (c + k % 2) % 2
        dev = (i2, at(i, yl, c2))
        if k == 0:
            send_if(jnp.logical_not(self_out), ws.at[c2], wo.at[slot], wor.at[slot], dev)
        else:
            send(ws.at[c2], wo.at[slot], wor.at[slot], dev)

    @pl.when(self_out)
    def _():
        wo[slot] = ws[c]

    x_late(4)
    x_other_core(2)
    compute(2)
    x_other_core(3)
    compute(3)
    x_other_core(4)
    compute(4)

    def normalise(r, carry):
        rows = pl.ds(pl.multiple_of(r * 128, 128), 128)
        into = pl.ds(pl.multiple_of(8 + r * 128, 8), 128)
        total = jnp.sum(ssq[rows, :], axis=1, keepdims=True)
        inverse = lax.rsqrt(total * (1.0 / D) + 1e-06)
        ext[:, into, :] = (ext[:, into, :] * inverse[None]).astype(BF16).astype(F32)
        return carry

    lax.fori_loop(0, T // 128, normalise, 0)
    send_if(i < NI - 1, ext.at[:, pl.ds(T, 8)], ext.at[:, pl.ds(0, 8)], hr, ((i + 1) % NI, j))

    rate_t, resid_t = rate[...].T, resid[...].T
    scale_t = jnp.sqrt(one_minus_exp_neg(2.0 * rate_t))
    weight_t = resid_t * scale_t
    lam_t = jnp.exp(-rate_t)

    def wide(table, n):
        return jnp.broadcast_to(table[n:n + 1, :], (CH, F))

    lam = [wide(lam_t, n) for n in range(ORDER)]
    tap = lambda t, q: jnp.broadcast_to(filt[t, q:q + 1, :], (CH, F))

    @pl.when(i == 0)
    def _():
        ext[:, 0:8, :] = tail[...]

    @pl.when(i > 0)
    def _():
        arrived(ext.at[:, pl.ds(0, 8)], hr)

    def chunk_rows(start, q):
        return ext[q, pl.ds(start, CH, stride=CL), :]

    kt, vt = [tap(t, 1) for t in range(3)], [tap(t, 2) for t in range(3)]
    U = 4

    def first(it, carry):
        k1, k2, v1, v2 = carry[:4]
        state = list(carry[4:])
        for u in range(U):
            s = it * U + u
            k0, v0 = chunk_rows(8 + s, 1), chunk_rows(8 + s, 2)
            keys = kt[0] * k0 + kt[1] * k1 + kt[2] * k2
            values = vt[0] * v0 + vt[1] * v1 + vt[2] * v2
            m = (keys * values).astype(BF16).astype(F32)
            mx[s] = m
            state = [lam[n] * state[n] + m for n in range(ORDER)]
            k1, k2, v1, v2 = k0, k1, v0, v1
        return (k1, k2, v1, v2, *state)

    zero = jnp.zeros((CH, F), F32)
    carry = lax.fori_loop(
        0, CL // U, first,
        (chunk_rows(7, 1), chunk_rows(6, 1), chunk_rows(7, 2), chunk_rows(6, 2)) + (zero,) * ORDER,
    )
    row8 = lax.broadcasted_iota(jnp.int32, (CH, F), 0)
    for n in range(ORDER):
        total, r = carry[4 + n], jnp.broadcast_to(rate_t[n:n + 1, :], (CH, F))
        for shift in (1, 2, 4):
            moved = jnp.where(row8 >= shift, pltpu.roll(total, shift, axis=0), 0.0)
            total = total + jnp.exp(-r * float(CL * shift)) * moved
        ts[n] = total
        endb[n:n + 1, :] = total[CH - 1:CH, :]
    ends[i] = endb[...]
    for k in range(1, NI):
        send(endb, ends.at[i], er.at[i], ((i + k) % NI, j))
    start_t = st_in[...].T / scale_t
    whole = jnp.exp(-rate_t * float(T))
    for k in range(1, NI):
        arrived(ends.at[(i + k) % NI], er.at[(i + k) % NI])
    now, mine = start_t, start_t
    for k in range(NI):
        mine = jnp.where(i == k, now, mine)
        now = whole * now + ends[k]
    st_out[...] = (now * scale_t).T

    qt = [tap(t, 0) for t in range(3)]
    weight = [wide(weight_t, n) for n in range(ORDER)]
    direct = jnp.broadcast_to(skip[...], (CH, F))
    chunk_start = row8.astype(F32) * float(CL)
    entering = []
    for n in range(ORDER):
        r = jnp.broadcast_to(rate_t[n:n + 1, :], (CH, F))
        before = jnp.where(row8 >= 1, pltpu.roll(ts[n], 1, axis=0), 0.0)
        entering.append(before + jnp.exp(-r * chunk_start) * jnp.broadcast_to(mine[n:n + 1, :], (CH, F)))

    def second(it, carry):
        q1, q2 = carry[:2]
        state = list(carry[2:])
        for u in range(U):
            s = it * U + u
            q0 = chunk_rows(8 + s, 0)
            query = qt[0] * q0 + qt[1] * q1 + qt[2] * q2
            m = mx[s]
            state = [lam[n] * state[n] + m for n in range(ORDER)]
            terms = [weight[n] * state[n] for n in range(ORDER)] + [direct * m]
            while len(terms) > 1:
                terms = [a + b for a, b in zip(terms[::2], terms[1::2])] + terms[len(terms) & ~1:]
            gf[pl.ds(s, CH, stride=CL), :] = query * terms[0]
            q1, q2 = q0, q1
        return (q1, q2, *state)

    lax.fori_loop(0, CL // U, second, (chunk_rows(7, 0), chunk_rows(6, 0), *entering))

    own = z * 2 + c
    for h in range(2):
        gg[h, own] = gf[h * H:(h + 1) * H, :].astype(BF16)

    def g_send(h, ss, dev):
        send(gg.at[h, ss], gg.at[h, ss], gr.at[h, ss], dev)

    def g_wait(h, ss):
        arrived(gg.at[h, ss], gr.at[h, ss])

    for h in range(2):
        g_send(h, own, dev_up)
        g_send(h, own, dev_down)
        g_send(h, own, dev_c)

    pl.when(jnp.logical_not(self_out))(lambda: arrived(wo.at[slot], wor.at[slot]))
    for k in range(1, 16):
        src = ((z + k // 2) % NZ) * 2 + (c + k % 2) % 2
        arrived(wo.at[src], wor.at[src])

    def clear_acc(r, carry):
        acc[pl.ds(r * 128, 128), :] = jnp.zeros((128, 2 * F), F32)
        return carry

    lax.fori_loop(0, T // 128, clear_acc, 0)

    def g_step(s):
        for plus in (True, False):
            zo = (z + NZ - s) % NZ if plus else (z + s) % NZ
            dev = dev_up if plus else dev_down
            for h in range(2):
                hops = 4 if plus == (h == 0) else 3
                if s > hops:
                    continue
                g_wait(h, zo * 2 + c)
                if s < hops:
                    g_send(h, zo * 2 + c, dev)
                g_send(h, zo * 2 + c, dev_c)

    def g_compute(s):
        origins = ((z + NZ - s) % NZ, (z + s) % NZ)[: 1 if s in (0, NZ // 2) else 2]
        for zo in origins:
            for h in range(2):
                g_wait(h, zo * 2 + 1 - c)

        def body(k, carry):
            zo = (z + NZ - s + (k // 4) * 2 * s) % NZ
            r = k % 4
            h, rows = r // 2, pl.ds(pl.multiple_of((r % 2) * TILE, TILE), TILE)
            total = pl.ds(pl.multiple_of(r * TILE, TILE), TILE)
            left = jnp.concatenate([gg[h, zo * 2, rows, :], gg[h, zo * 2 + 1, rows, :]], axis=1)
            right = jnp.concatenate(
                [jnp.concatenate([wo[zo * 2 + cc, 0], wo[zo * 2 + cc, 1]], axis=1) for cc in range(2)], axis=0
            )
            acc[total, :] += jnp.dot(left, right, preferred_element_type=F32)
            return carry

        lax.fori_loop(0, 4 * len(origins), body, 0)

    g_step(1)
    g_compute(0)
    g_step(2)
    g_compute(1)
    g_step(3)
    g_compute(2)
    g_step(4)
    g_compute(3)
    g_compute(4)

    for h in range(2):
        osend[h] = acc[h * H:(h + 1) * H, F:2 * F].astype(BF16)
        send(osend.at[h], orecv.at[h], orr.at[h], dev_y)
    for h in range(2):
        arrived(orecv.at[h], orr.at[h])
        rows = slice(h * H, (h + 1) * H)
        out[rows, :] = (act[rows, :].astype(F32) + (acc[rows, 0:F] + orecv[h].astype(F32))).astype(BF16)

    for copy, cond in sends:
        if cond is None:
            copy.wait_send()
        else:
            pl.when(cond)(lambda copy=copy: copy.wait_send())


def local(activations, norm_gain, w_in, tail_rows, short_filter, decay_rate, residue, skip_gain, state_in, w_out):
    tail = jnp.pad(tail_rows.transpose(0, 2, 1).astype(F32), ((0, 0), (6, 0), (0, 0)))
    vmem = pl.BlockSpec(memory_space=pltpu.VMEM)
    dma = pltpu.SemaphoreType.DMA
    return pl.pallas_call(
        block_kernel,
        out_shape=(jax.ShapeDtypeStruct((T, F), BF16), jax.ShapeDtypeStruct((F, ORDER), F32)),
        in_specs=[vmem] * 10,
        out_specs=(vmem, vmem),
        scratch_shapes=[
            pltpu.VMEM((2, NJ, HG, F), BF16),
            pltpu.VMEM((NI, 2, 256, 3 * F), BF16),
            pltpu.VMEM((3, T + 8, F), F32),
            pltpu.VMEM((T, F), F32),
            pltpu.VMEM((CL, CH, F), F32),
            pltpu.VMEM((ORDER, CH, F), F32),
            pltpu.VMEM((ORDER, F), F32),
            pltpu.VMEM((NI, ORDER, F), F32),
            pltpu.VMEM((T, F), F32),
            pltpu.VMEM((2, 16, H, F), BF16),
            pltpu.VMEM((2, 2, F, F), BF16),
            pltpu.VMEM((16, 2, F, F), BF16),
            pltpu.VMEM((T, 2 * F), F32),
            pltpu.VMEM((2, H, F), BF16),
            pltpu.VMEM((2, H, F), BF16),
            dma((N_SEND,)),
            dma((2, NJ)),
            dma((NI, 2)),
            dma,
            dma((NI,)),
            dma((16,)),
            dma((2, 16)),
            dma((2,)),
        ],
        compiler_params=pltpu.CompilerParams(
            collective_id=0, has_side_effects=True, vmem_limit_bytes=56 << 20
        ),
    )(
        activations, norm_gain.reshape(1, F), w_in.reshape(512, 3 * F), tail, short_filter,
        decay_rate, residue, skip_gain.reshape(1, F), state_in, w_out,
    )


def solution(mesh):
    placed = (
        P("ctx", "mp"),
        P("mp"),
        P("ctx", None, "mp"),
        P(None, "mp", None),
        P(None, None, "mp"),
        P("mp", None),
        P("mp", None),
        P("mp"),
        P("mp", None),
        P("mp", "ctx"),
    )
    return jax.shard_map(
        local, mesh=mesh, in_specs=placed, out_specs=(P("ctx", "mp"), P("mp", None)), check_vma=False
    )
```

time: 459 us -> 198 us (0.43)
  waiting for transfers between devices: 211 us -> 0 us
  Pallas kernels: 0 us -> 186 us
  blocking collectives: 97.1 us -> 0 us
  local copies, waits for them, and re-layouts: 85.8 us -> 8.14 us
  matrix products: 19.3 us -> 0 us
  other arithmetic: 17.2 us -> 0.6 us
  between operations: 14.5 us -> 0.66 us
  starting transfers between devices: 11.3 us -> 0 us
    pallas_call x0 -> x1, Pallas kernels: none -> 186 us  [local(): pl.pallas_call(block_kernel, out_shape=(jax.ShapeDtypeStruct((T, F), BF16...]
    all_gather x3 -> x0, waiting for transfers between devices: 107 us -> none  [the longest x1 92.1 us: local(): lax.all_gather(normed, 'mp', axis=1, tiled=True)]
    unnamed x5 -> x0, waiting for transfers between devices: 98.1 us -> none
    psum x1 -> x0, blocking collectives: 57.5 us -> none  [local(): squares = lax.psum(jnp.sum(act_float * act_float, axis=1), 'mp')]
    all_gather x1 -> x0, blocking collectives: 28.2 us -> none  [local(): final_state = lax.all_gather(final_part, 'ctx', axis=0, tiled=True)]
    pad x12 -> x0, local copies, waits for them, and re-layouts: 26.4 us -> none  [modal_conv(): lax.associative_scan(chain_step, (decays, loading), axis=1)]
    slice x20 -> x0, local copies, waits for them, and re-layouts: 20.3 us -> none  [the longest x19 20.2 us: modal_conv(): lax.associative_scan(chain_step, (decays, loading), axis=1)]
    dot_general x7 -> x0, matrix products: 19.3 us -> none  [the longest x1 7.72 us: local(): lax.dot_general(panel, lax.all_gather(normed, 'mp', axis=1, tiled=True),...]
  transfers between devices with their start and end apart: 6 -> 0, of which waited for: 5 -> 0; matrix products, arithmetic and copies ran while one was open for 22% -> 0% of each run, Pallas kernels for 0% -> 0%
where the time goes in v1:
time: 198 us; the launch traced here: 195 us
  Pallas kernels  186 us (94%)
  local copies, waits for them, and re-layouts  8.14 us (4%)
    pallas_call x1, Pallas kernels, local(): pl.pallas_call(block_kernel, out_shape=(jax.ShapeDtypeStruct((T, F), BF16...  186 us
    unnamed x13, local copies, waits for them, and re-layouts  5.71 us

profile of v1, /device:TPU:1, one launch (start us, length us, event | category | flops | bytes accessed | tf_op | source)
XLA Modules:
  0.0 195.3 jit_solution(13284639434857331381)
XLA Ops:
  0.6 1.2 copy.17
  1.8 0.0 copy-start
  1.8 0.9 copy.18.w_local
  2.7 0.0 copy-done
  2.7 0.0 copy-start.1
  2.7 0.7 copy.19.rate
  3.5 0.0 copy-done.1
  3.5 0.0 copy-start.2
  3.5 0.7 copy.20.resid
  4.2 0.0 copy-done.2
  4.2 0.7 copy.21.st_in
  4.9 0.0 copy-start.3
  4.9 0.7 copy-done.3
  5.6 0.6 pad_convert_fusion.tail
  6.2 185.9 %shard_map.113 = (bf16[1024,128]{1,0:T(8,128)(2,1)}, f32[128,16]{1,0:T(8,128)}) custom-call(bf16[1024,128]{1,0:T(8,128)(2,1)} %act.1, f32[1,128]{1,0:T(1,128)} %bitcast.6, bf16[512,384]{1,0:T(8,128)(2,1)} %copy.18.w_local, f32[3,8,128]{2,1,0:T(8,128)} %pad_convert_fusion.tail, f32[3,3,128]{2,1,0:T(4,128)} %filt.1, f32[128,16]{1,0:T(8,128)} %copy.19.rate, ...), custom_call_target="tpu_custom_call" | custom-call | tf_op jit(solution)/shard_map/pallas_call | solution.py:455
  192.1 1.5 copy.22
  193.6 1.7 copy.24
Async XLA Ops:
  1.8 0.9 copy-start
  2.7 0.7 copy-start.1
  3.5 0.7 copy-start.2
  4.9 0.7 copy-start.3

commit v2 on v1

v2 whole, which is shorter than its diff:
```python
import jax
import jax.numpy as jnp
from jax import lax
from jax.experimental import pallas as pl
from jax.experimental.pallas import tpu as pltpu
from jax.sharding import PartitionSpec as P

MESH = pl.DeviceIdType.MESH
F32, BF16 = jnp.float32, jnp.bfloat16

NI, NJ = 8, 32
NZ, NX = 8, 4
T, F, D, ORDER = 1024, 128, 4096, 16
H = T // 2
HG = H + 16
CH = 8
CL = T // CH
N_SEND = 176
PLUS_HOPS = {"own0": 4, "own1": 3, "par1": 4}
MINUS_HOPS = {"own0": 3, "own1": 4, "par1": 4}


def one_minus_exp_neg(v):
    series = 1.0 - v * (1.0 / 8.0)
    for k in (7, 6, 5, 4, 3, 2):
        series = 1.0 - v * (1.0 / k) * series
    return v * series


def block_kernel(
    act, gain, w_local, tail, filt, rate, resid, skip, st_in, wout,
    out, st_out,
    xg, xs, wg, wt, ext, ssq, mx, ts, endb, ends, gf, gk, ws, wo, pa, sb, rb,
    ssem, xr, wr, wtr, hr, er, wor, gr, rr,
):
    i, j = lax.axis_index("ctx"), lax.axis_index("mp")
    z, yl, c = j // 4, (j // 2) % 2, j % 2
    at = lambda zz, yy, cc: zz * 4 + yy * 2 + cc
    up, down = (z + 1) % NZ, (z + NZ - 1) % NZ
    dev_up, dev_down = (i, at(up, yl, c)), (i, at(down, yl, c))
    dev_y, dev_c = (i, at(z, 1 - yl, c)), (i, at(z, yl, 1 - c))
    ix_up, ix_down = (i + 2) % NI, (i + NI - 2) % NI
    pair = i + 1 - 2 * (i % 2)
    dev_xu, dev_xd, dev_yh = (ix_up, j), (ix_down, j), (pair, j)
    y = (i % 2) * 2 + yl
    yu, yd = (y + 1) % 4, (y + 3) % 4
    i_yu, i_yd = (i // 2) * 2 + yu // 2, (i // 2) * 2 + yd // 2
    dev_yu, dev_yd = (i_yu, at(z, yu % 2, c)), (i_yd, at(z, yd % 2, c))
    dev_yc = (i, at(z, 1 - yl, 1 - c))

    sends = []

    def send(src, dst, recv_sem, dev):
        copy = pltpu.make_async_remote_copy(
            src_ref=src, dst_ref=dst, send_sem=ssem.at[len(sends)], recv_sem=recv_sem,
            device_id=dev, device_id_type=MESH,
        )
        sends.append((copy, None))
        copy.start()

    def send_if(cond, src, dst, recv_sem, dev):
        copy = pltpu.make_async_remote_copy(
            src_ref=src, dst_ref=dst, send_sem=ssem.at[len(sends)], recv_sem=recv_sem,
            device_id=dev, device_id_type=MESH,
        )
        sends.append((copy, cond))
        pl.when(cond)(lambda: copy.start())

    def arrived(dst, recv_sem):
        pltpu.make_async_remote_copy(
            src_ref=dst, dst_ref=dst, send_sem=ssem.at[0], recv_sem=recv_sem,
            device_id=dev_up, device_id_type=MESH,
        ).wait_recv()

    barrier = pltpu.get_barrier_semaphore()

    def tell(dev):
        pl.semaphore_signal(barrier, inc=1, device_id=dev, device_id_type=MESH)

    for dev in (dev_up, dev_down, dev_c, dev_yu, dev_yd, dev_yc):
        tell(dev)
    for k in range(1, NI):
        tell(((i + k) % NI, j))

    g = gain[...]
    g_hi = g.astype(BF16)
    g_rest = g - g_hi.astype(F32)
    g_mid = g_rest.astype(BF16)
    g_lo = (g_rest - g_mid.astype(F32)).astype(BF16)
    row16 = lax.broadcasted_iota(jnp.int32, (16, F), 0)
    zero16 = jnp.zeros((16, F), F32)
    g_rows = jnp.where(
        row16 == 0, g_hi.astype(F32) + zero16,
        jnp.where(row16 == 1, g_mid.astype(F32) + zero16,
                  jnp.where(row16 == 2, g_lo.astype(F32) + zero16, zero16)),
    ).astype(BF16)
    for h in range(2):
        xg[h, j, 0:H, :] = act[h * H:(h + 1) * H, :]
        xg[h, j, H:HG, :] = g_rows
    for half in range(2):
        wg[i, half] = w_local[:, half * 256:(half + 1) * 256, :]
    for k in range(4):
        ws[k] = wout[:, k * F:(k + 1) * F]
    wo[i, yl, pl.ds(pl.multiple_of(c * F, F), F), :] = ws[yl * 2 + c]

    pl.semaphore_wait(barrier, 6 + NI - 1)

    def x_send(h, jj, dev):
        send(xg.at[h, jj], xg.at[h, jj], xr.at[h, jj], dev)

    def x_wait(h, jj):
        arrived(xg.at[h, jj], xr.at[h, jj])

    def w_send(ii, half, dev):
        send(wg.at[ii, half], wg.at[ii, half], wr.at[ii, half], dev)

    def w_wait(ii, half):
        arrived(wg.at[ii, half], wr.at[ii, half])

    for h in range(2):
        x_send(h, j, dev_y)
        x_send(h, j, dev_up)
        x_send(h, j, dev_down)
        x_send(h, j, dev_c)
    send(wg.at[i, 0], wt.at[0], wtr.at[0], dev_yu)
    send(wg.at[i, 1], wt.at[1], wtr.at[1], dev_yd)
    for half in range(2):
        w_send(i, half, dev_xu)
        w_send(i, half, dev_xd)

    mine_rows = pl.ds(pl.multiple_of(c * F, F), F)
    for dev, block in ((dev_c, yl * 2 + 1 - c), (dev_y, (1 - yl) * 2 + c), (dev_yc, (1 - yl) * 2 + 1 - c)):
        send(ws.at[block], wo.at[i, yl, mine_rows, :], wor.at[i, yl, c], dev)

    def clear(r, carry):
        ext[:, pl.ds(8 + r * 128, 128), :] = jnp.zeros((3, 128, F), F32)
        ssq[pl.ds(r * 128, 128), :] = jnp.zeros((128, F), F32)
        return carry

    lax.fori_loop(0, T // 128, clear, 0)

    jp = at(z, 1 - yl, c)
    x_wait(1, jp)
    x_send(1, jp, dev_up)
    x_send(1, jp, dev_down)
    x_send(1, jp, dev_c)
    x_wait(0, jp)
    x_send(0, jp, dev_c)
    arrived(wt.at[0], wtr.at[0])
    send(wt.at[0], wg.at[i_yd, 0], wr.at[i_yd, 0], dev_yu)
    arrived(wt.at[1], wtr.at[1])
    send(wt.at[1], wg.at[i_yu, 1], wr.at[i_yu, 1], dev_yd)
    for half in range(2):
        w_wait(pair, half)
        w_send(pair, half, dev_xu)
        w_send(pair, half, dev_xd)

    def x_step(s):
        for plus in (True, False):
            zo = (z + NZ - s) % NZ if plus else (z + s) % NZ
            hops = PLUS_HOPS if plus else MINUS_HOPS
            dev = dev_up if plus else dev_down
            for name, h, yy in (("own0", 0, yl), ("own1", 1, yl), ("par1", 1, 1 - yl)):
                if s > hops[name]:
                    continue
                jj = at(zo, yy, c)
                if name == "par1" and s == 4:
                    if plus:
                        x_wait(h, jj)
                        x_send(h, jj, dev_c)
                    continue
                x_wait(h, jj)
                if name == "par1" and s == 3:
                    send_if(c == (0 if plus else 1), xg.at[h, jj], xg.at[h, jj], xr.at[h, jj], dev)
                elif s < hops[name]:
                    x_send(h, jj, dev)
                if name == "own0":
                    x_send(h, jj, dev_y)
                x_send(h, jj, dev_c)

    def x_late(s):
        for zo in ((z + NZ - s) % NZ, (z + s) % NZ)[: 1 if s == NZ // 2 else 2]:
            jj = at(zo, 1 - yl, c)
            x_wait(0, jj)
            x_send(0, jj, dev_c)

    def x_other_core(s):
        for zo in ((z + NZ - s) % NZ, (z + s) % NZ)[: 1 if s in (0, NZ // 2) else 2]:
            for yy in range(2):
                for h in range(2):
                    x_wait(h, at(zo, yy, 1 - c))

    def origin(s, k):
        return (z + NZ - s + k * 2 * s) % NZ

    def n_origins(s):
        return 1 if s in (0, NZ // 2) else 2

    def prepare(s):
        x_other_core(s)

        def body(k, carry):
            zo, h, r = origin(s, k // 8), (k // 4) % 2, k % 4
            rows = pl.ds(pl.multiple_of(r * 128, 128), 128)
            squares = None
            for b in range(4):
                jj = zo * 4 + b
                block = xg[h, jj, rows, :].astype(F32)
                gains = jnp.sum(xg[h, jj, pl.ds(H, 16), :].astype(F32), axis=0, keepdims=True)
                xs[h, zo, rows, b * F:(b + 1) * F] = (block * gains).astype(BF16)
                squares = block * block if squares is None else squares + block * block
            ssq[pl.ds(pl.multiple_of(h * H + r * 128, 128), 128), :] += squares
            return carry

        lax.fori_loop(0, 8 * n_origins(s), body, 0)

    def multiply(s):
        def body(k, carry):
            zo, h = origin(s, k // 2), k % 2
            into = pl.ds(pl.multiple_of(8 + h * H, 8), H)
            right = jnp.concatenate(
                [jnp.concatenate([wg[zo, half, q] for half in range(2)], axis=0) for q in range(3)], axis=1
            )
            product = jnp.dot(xs[h, zo], right, preferred_element_type=F32)
            for q in range(3):
                ext[q, into, :] += product[:, q * F:(q + 1) * F]
            return carry

        lax.fori_loop(0, 2 * n_origins(s), body, 0)

    def o_send(ii, half, dev):
        send(wo.at[ii, half], wo.at[ii, half], wor.at[ii, half, 0], dev)

    def o_wait(ii, half):
        arrived(wo.at[ii, half], wor.at[ii, half, 0])

    pd, pu = (pair + NI - 2) % NI, (pair + 2) % NI
    far, pfar = (i + 4) % NI, (pair + 4) % NI

    def pass_on(wait, forward, below, above):
        for half in (0, 1):
            wait(below, half)
            if half == 0:
                forward(below, 0, dev_xu)
            wait(above, half)
            if half == 1:
                forward(above, 1, dev_xd)

    x_step(1)
    pass_on(w_wait, w_send, ix_down, ix_up)
    prepare(0)
    x_step(2)
    x_late(1)
    pass_on(w_wait, w_send, pd, pu)
    prepare(1)
    for yy, cc in ((yl, 1 - c), (1 - yl, c), (1 - yl, 1 - c)):
        rows = pl.ds(pl.multiple_of(cc * F, F), F)
        arrived(wo.at[i, yy, rows, :], wor.at[i, yy, cc])
    for half in range(2):
        for dev in (dev_yh, dev_xu, dev_xd):
            o_send(i, half, dev)
    x_step(3)
    x_late(2)
    prepare(2)
    for half in range(2):
        w_wait(far, half)
    for half in range(2):
        w_wait(pfar, half)
    multiply(0)
    multiply(1)
    x_step(4)
    for half in range(2):
        o_wait(pair, half)
        for dev in (dev_xu, dev_xd):
            o_send(pair, half, dev)
    x_late(3)
    prepare(3)
    multiply(2)
    x_late(4)
    pass_on(o_wait, o_send, ix_down, ix_up)
    multiply(3)
    prepare(4)
    multiply(4)
    pass_on(o_wait, o_send, pd, pu)

    def normalise(r, carry):
        rows = pl.ds(pl.multiple_of(r * 128, 128), 128)
        into = pl.ds(pl.multiple_of(8 + r * 128, 8), 128)
        total = jnp.sum(ssq[rows, :], axis=1, keepdims=True)
        inverse = lax.rsqrt(total * (1.0 / D) + 1e-06)
        ext[:, into, :] = (ext[:, into, :] * inverse[None]).astype(BF16).astype(F32)
        return carry

    lax.fori_loop(0, T // 128, normalise, 0)
    send_if(i < NI - 1, ext.at[:, pl.ds(T, 8)], ext.at[:, pl.ds(0, 8)], hr, ((i + 1) % NI, j))

    rate_t, resid_t = rate[...], resid[...]
    scale_t = jnp.sqrt(one_minus_exp_neg(2.0 * rate_t))
    weight_t = resid_t * scale_t
    lam_t = jnp.exp(-rate_t)

    def wide(table, n):
        return jnp.broadcast_to(table[n:n + 1, :], (CH, F))

    lam = [wide(lam_t, n) for n in range(ORDER)]
    tap = lambda t, q: jnp.broadcast_to(filt[t, q:q + 1, :], (CH, F))

    @pl.when(i == 0)
    def _():
        ext[:, 6:8, :] = tail[...].astype(F32)

    @pl.when(i > 0)
    def _():
        arrived(ext.at[:, pl.ds(0, 8)], hr)

    def chunk_rows(start, q):
        return ext[q, pl.ds(start, CH, stride=CL), :]

    kt, vt = [tap(t, 1) for t in range(3)], [tap(t, 2) for t in range(3)]
    U = 4

    def first(it, carry):
        k1, k2, v1, v2 = carry[:4]
        state = list(carry[4:])
        for u in range(U):
            s = it * U + u
            k0, v0 = chunk_rows(8 + s, 1), chunk_rows(8 + s, 2)
            keys = kt[0] * k0 + kt[1] * k1 + kt[2] * k2
            values = vt[0] * v0 + vt[1] * v1 + vt[2] * v2
            m = (keys * values).astype(BF16).astype(F32)
            mx[s] = m
            state = [lam[n] * state[n] + m for n in range(ORDER)]
            k1, k2, v1, v2 = k0, k1, v0, v1
        return (k1, k2, v1, v2, *state)

    zero = jnp.zeros((CH, F), F32)
    carry = lax.fori_loop(
        0, CL // U, first,
        (chunk_rows(7, 1), chunk_rows(6, 1), chunk_rows(7, 2), chunk_rows(6, 2)) + (zero,) * ORDER,
    )
    row8 = lax.broadcasted_iota(jnp.int32, (CH, F), 0)
    for n in range(ORDER):
        total, r = carry[4 + n], jnp.broadcast_to(rate_t[n:n + 1, :], (CH, F))
        for shift in (1, 2, 4):
            moved = jnp.where(row8 >= shift, pltpu.roll(total, shift, axis=0), 0.0)
            total = total + jnp.exp(-r * float(CL * shift)) * moved
        ts[n] = total
        endb[n:n + 1, :] = total[CH - 1:CH, :]
    ends[i] = endb[...]
    for k in range(1, NI):
        send(endb, ends.at[i], er.at[i], ((i + k) % NI, j))
    start_t = st_in[...] / scale_t
    whole = jnp.exp(-rate_t * float(T))
    for k in range(1, NI):
        arrived(ends.at[(i + k) % NI], er.at[(i + k) % NI])
    now, mine = start_t, start_t
    for k in range(NI):
        mine = jnp.where(i == k, now, mine)
        now = whole * now + ends[k]
    st_out[...] = now * scale_t

    qt = [tap(t, 0) for t in range(3)]
    weight = [wide(weight_t, n) for n in range(ORDER)]
    direct = jnp.broadcast_to(skip[...], (CH, F))
    chunk_start = row8.astype(F32) * float(CL)
    entering = []
    for n in range(ORDER):
        r = jnp.broadcast_to(rate_t[n:n + 1, :], (CH, F))
        before = jnp.where(row8 >= 1, pltpu.roll(ts[n], 1, axis=0), 0.0)
        entering.append(before + jnp.exp(-r * chunk_start) * jnp.broadcast_to(mine[n:n + 1, :], (CH, F)))

    def second(it, carry):
        q1, q2 = carry[:2]
        state = list(carry[2:])
        for u in range(U):
            s = it * U + u
            q0 = chunk_rows(8 + s, 0)
            query = qt[0] * q0 + qt[1] * q1 + qt[2] * q2
            m = mx[s]
            state = [lam[n] * state[n] + m for n in range(ORDER)]
            terms = [weight[n] * state[n] for n in range(ORDER)] + [direct * m]
            while len(terms) > 1:
                terms = [a + b for a, b in zip(terms[::2], terms[1::2])] + terms[len(terms) & ~1:]
            gf[pl.ds(s, CH, stride=CL), :] = query * terms[0]
            q1, q2 = q0, q1
        return (q1, q2, *state)

    lax.fori_loop(0, CL // U, second, (chunk_rows(7, 0), chunk_rows(6, 0), *entering))

    def g_send(h, yy, dev):
        send(gk.at[h, yy * 2 + c], gk.at[h, yy * 2 + c], gr.at[h, yy * 2 + c], dev)

    def g_wait(h, slot):
        arrived(gk.at[h, slot], gr.at[h, slot])

    for h in range(2):
        gk[h, yl * 2 + c] = gf[h * H:(h + 1) * H, :].astype(BF16)
        g_send(h, yl, dev_y)
        g_send(h, yl, dev_c)
    for half in range(2):
        o_wait(far, half)
        o_wait(pfar, half)
    for h in range(2):
        g_wait(h, (1 - yl) * 2 + c)
        g_send(h, 1 - yl, dev_c)

    def partial(h, first_to, second_to):
        left = jnp.concatenate([gk[h, slot] for slot in range(4)], axis=1)
        right = jnp.concatenate(
            [jnp.concatenate([wo[to, half] for half in range(2)], axis=0) for to in (first_to, second_to)], axis=1
        )
        product = jnp.dot(left, right, preferred_element_type=F32)
        pa[h, first_to] = product[:, 0:F]
        pa[h, second_to] = product[:, F:2 * F]

    steps = {(d, h): 4 if d == h else 3 for d in range(2) for h in range(2)}

    def target(d, h, s):
        n = steps[d, h]
        return (z + n - s) % NZ if d == 0 else (z + NZ - n + s) % NZ

    def pass_sum(d, h, s):
        total = pa[h, target(d, h, s)]
        if s > 0:
            arrived(rb.at[d, h, s - 1], rr.at[d, h, s - 1])
            total = total + rb[d, h, s - 1].astype(F32)
        sb[d, h, s] = total.astype(BF16)
        send(sb.at[d, h, s], rb.at[d, h, s], rr.at[d, h, s], dev_up if d == 0 else dev_down)

    for h in range(2):
        g_wait(h, yl * 2 + 1 - c)
        g_wait(h, (1 - yl) * 2 + 1 - c)
        partial(h, target(0, h, 0), target(1, h, 0))
        pass_sum(0, h, 0)
        pass_sum(1, h, 0)
    for h in range(2):
        partial(h, target(0, h, 1), target(1, h, 1))
    for h in range(2):
        partial(h, target(0, h, 2), target(1, h, 2))
        partial(h, target(h, h, 3), z)
    for s in range(1, 4):
        for h in range(2):
            for d in range(2):
                if s < steps[d, h]:
                    pass_sum(d, h, s)
    for h in range(2):
        rows = slice(h * H, (h + 1) * H)
        total = pa[h, z] + act[rows, :].astype(F32)
        for d in range(2):
            last = steps[d, h] - 1
            arrived(rb.at[d, h, last], rr.at[d, h, last])
            total = total + rb[d, h, last].astype(F32)
        out[rows, :] = total.astype(BF16)

    for copy, cond in sends:
        if cond is None:
            copy.wait_send()
        else:
            pl.when(cond)(lambda copy=copy: copy.wait_send())


def local(activations, norm_gain, w_in, tail_rows, short_filter, decay_rate, residue, skip_gain, state_in, w_out):
    vmem = pl.BlockSpec(memory_space=pltpu.VMEM)
    dma = pltpu.SemaphoreType.DMA
    block_out, state_out = pl.pallas_call(
        block_kernel,
        out_shape=(jax.ShapeDtypeStruct((T, F), BF16), jax.ShapeDtypeStruct((ORDER, F), F32)),
        in_specs=[vmem] * 10,
        out_specs=(vmem, vmem),
        scratch_shapes=[
            pltpu.VMEM((2, NJ, HG, F), BF16),
            pltpu.VMEM((2, NZ, H, 4 * F), BF16),
            pltpu.VMEM((NI, 2, 3, 256, F), BF16),
            pltpu.VMEM((2, 3, 256, F), BF16),
            pltpu.VMEM((3, T + 8, F), F32),
            pltpu.VMEM((T, F), F32),
            pltpu.VMEM((CL, CH, F), F32),
            pltpu.VMEM((ORDER, CH, F), F32),
            pltpu.VMEM((ORDER, F), F32),
            pltpu.VMEM((NI, ORDER, F), F32),
            pltpu.VMEM((T, F), F32),
            pltpu.VMEM((2, 4, H, F), BF16),
            pltpu.VMEM((4, F, F), BF16),
            pltpu.VMEM((NI, 2, 2 * F, F), BF16),
            pltpu.VMEM((2, NZ, H, F), F32),
            pltpu.VMEM((2, 2, 4, H, F), BF16),
            pltpu.VMEM((2, 2, 4, H, F), BF16),
            dma((N_SEND,)),
            dma((2, NJ)),
            dma((NI, 2)),
            dma((2,)),
            dma,
            dma((NI,)),
            dma((NI, 2, 2)),
            dma((2, 4)),
            dma((2, 2, 4)),
        ],
        compiler_params=pltpu.CompilerParams(
            collective_id=0, has_side_effects=True, vmem_limit_bytes=56 << 20
        ),
    )(
        activations, norm_gain.reshape(1, F), w_in.transpose(1, 0, 2), tail_rows.transpose(0, 2, 1), short_filter,
        decay_rate.T, residue.T, skip_gain.reshape(1, F), state_in.T, w_out,
    )
    return block_out, state_out.T


def solution(mesh):
    placed = (
        P("ctx", "mp"),
        P("mp"),
        P("ctx", None, "mp"),
        P(None, "mp", None),
        P(None, None, "mp"),
        P("mp", None),
        P("mp", None),
        P("mp"),
        P("mp", None),
        P("mp", "ctx"),
    )
    return jax.shard_map(
        local, mesh=mesh, in_specs=placed, out_specs=(P("ctx", "mp"), P("mp", None)), check_vma=False
    )
```

time: 198 us -> 109 us (0.55); the launches traced: 195 us -> 109 us
  Pallas kernels: 186 us -> 106 us
  local copies, waits for them, and re-layouts: 8.14 us -> 2.28 us
    pallas_call x1, Pallas kernels: 186 us -> 106 us  [local(): pl.pallas_call(block_kernel, out_shape=(jax.ShapeDtypeStruct((T, F), BF16...]
    unnamed x13 -> x4, local copies, waits for them, and re-layouts: 5.71 us -> 2.28 us
where the time goes in v2:
time: 109 us
  Pallas kernels  106 us (97%)
  local copies, waits for them, and re-layouts  2.28 us (2%)
    pallas_call x1, Pallas kernels, local(): pl.pallas_call(block_kernel, out_shape=(jax.ShapeDtypeStruct((T, F), BF16...  106 us
    unnamed x4, local copies, waits for them, and re-layouts  2.28 us

profile of v2, /device:TPU:1, one launch (start us, length us, event | category | flops | bytes accessed | tf_op | source)
XLA Modules:
  0.0 109.3 jit_solution(6981818631075891830)
XLA Ops:
  0.6 106.4 %shard_map.113 = (bf16[1024,128]{1,0:T(8,128)(2,1)}, f32[16,128]{1,0:T(8,128)}) custom-call(bf16[1024,128]{1,0:T(8,128)(2,1)} %act.1, f32[1,128]{1,0:T(1,128)} %bitcast.14, bf16[3,512,128]{2,1,0:T(8,128)(2,1)} %bitcast.8, bf16[3,2,128]{2,1,0:T(2,128)(2,1)} %bitcast.13, f32[3,3,128]{2,1,0:T(4,128)} %filt.1, f32[16,128]{1,0:T(8,128)} %bitcast.9, ...), custom_call_target="tpu_custom_call" | custom-call | tf_op jit(solution)/shard_map/pallas_call | solution.py:465
  107.0 0.0 copy-start
  107.0 1.7 %copy.14 = bf16[1024,128]{1,0:T(8,128)(2,1)} copy(bf16[1024,128]{1,0:T(8,128)(2,1)} %get-tuple-element.8) | data formatting | bytes 524288
  108.7 0.0 copy-done
  108.7 0.6 copy.15
Async XLA Ops:
  107.0 1.7 %copy-start = (f32[16,128]{1,0:T(8,128)S(1)}, f32[16,128]{1,0:T(8,128)}, u32[]{:S(2)}) copy-start(f32[16,128]{1,0:T(8,128)} %get-tuple-element.5) | copy-start | bytes 24580

commit v3 on v2

--- a/solution.py
+++ b/solution.py
@@ -12,10 +12,12 @@
 NZ, NX = 8, 4
 T, F, D, ORDER = 1024, 128, 4096, 16
 H = T // 2
-HG = H + 16
+PARTS = (384, 640)
+STARTS = (0, 384)
+GAIN_ROWS = 16
 CH = 8
 CL = T // CH
-N_SEND = 176
+GROUPS = {name: n for n, name in enumerate(("x0", "x1", "w", "o", "ws", "halo", "ends", "g", "sum"))}
 PLUS_HOPS = {"own0": 4, "own1": 3, "par1": 4}
 MINUS_HOPS = {"own0": 3, "own1": 4, "par1": 4}
 
@@ -30,8 +32,8 @@
 def block_kernel(
     act, gain, w_local, tail, filt, rate, resid, skip, st_in, wout,
     out, st_out,
-    xg, xs, wg, wt, ext, ssq, mx, ts, endb, ends, gf, gk, ws, wo, pa, sb, rb,
-    ssem, xr, wr, wtr, hr, er, wor, gr, rr,
+    xg, xs, wg, ext, ssq, mx, ts, endb, ends, gf, gk, ws, wo, pa, sb, rb,
+    ssem, xr, wr, hr, er, wor, gr, rr,
 ):
     i, j = lax.axis_index("ctx"), lax.axis_index("mp")
     z, yl, c = j // 4, (j // 2) % 2, j % 2
@@ -42,29 +44,23 @@
     ix_up, ix_down = (i + 2) % NI, (i + NI - 2) % NI
     pair = i + 1 - 2 * (i % 2)
     dev_xu, dev_xd, dev_yh = (ix_up, j), (ix_down, j), (pair, j)
-    y = (i % 2) * 2 + yl
-    yu, yd = (y + 1) % 4, (y + 3) % 4
-    i_yu, i_yd = (i // 2) * 2 + yu // 2, (i // 2) * 2 + yd // 2
-    dev_yu, dev_yd = (i_yu, at(z, yu % 2, c)), (i_yd, at(z, yd % 2, c))
+    dev_xf = ((i + 4) % NI, j)
     dev_yc = (i, at(z, 1 - yl, 1 - c))
 
-    sends = []
-
-    def send(src, dst, recv_sem, dev):
-        copy = pltpu.make_async_remote_copy(
-            src_ref=src, dst_ref=dst, send_sem=ssem.at[len(sends)], recv_sem=recv_sem,
+    def transfer(group, src, dst, recv_sem, dev):
+        return pltpu.make_async_remote_copy(
+            src_ref=src, dst_ref=dst, send_sem=ssem.at[GROUPS[group]], recv_sem=recv_sem,
             device_id=dev, device_id_type=MESH,
         )
-        sends.append((copy, None))
-        copy.start()
-
-    def send_if(cond, src, dst, recv_sem, dev):
-        copy = pltpu.make_async_remote_copy(
-            src_ref=src, dst_ref=dst, send_sem=ssem.at[len(sends)], recv_sem=recv_sem,
-            device_id=dev, device_id_type=MESH,
-        )
-        sends.append((copy, cond))
-        pl.when(cond)(lambda: copy.start())
+
+    counts = dict.fromkeys(GROUPS, 0)
+
+    def send(group, src, dst, recv_sem, dev):
+        counts[group] += 1
+        transfer(group, src, dst, recv_sem, dev).start()
+
+    def all_sent(group, refs):
+        transfer(group, refs, refs, hr, dev_up).wait_send()
 
     def arrived(dst, recv_sem):
         pltpu.make_async_remote_copy(
@@ -77,7 +73,7 @@
     def tell(dev):
         pl.semaphore_signal(barrier, inc=1, device_id=dev, device_id_type=MESH)
 
-    for dev in (dev_up, dev_down, dev_c, dev_yu, dev_yd, dev_yc):
+    for dev in (dev_up, dev_down, dev_c, dev_y, dev_yc):
         tell(dev)
     for k in range(1, NI):
         tell(((i + k) % NI, j))
@@ -95,24 +91,27 @@
                   jnp.where(row16 == 2, g_lo.astype(F32) + zero16, zero16)),
     ).astype(BF16)
     for h in range(2):
-        xg[h, j, 0:H, :] = act[h * H:(h + 1) * H, :]
-        xg[h, j, H:HG, :] = g_rows
+        xg[h, j, 0:PARTS[h], :] = act[STARTS[h]:STARTS[h] + PARTS[h], :]
+        xg[h, j, PARTS[h]:PARTS[h] + GAIN_ROWS, :] = g_rows
     for half in range(2):
         wg[i, half] = w_local[:, half * 256:(half + 1) * 256, :]
     for k in range(4):
         ws[k] = wout[:, k * F:(k + 1) * F]
     wo[i, yl, pl.ds(pl.multiple_of(c * F, F), F), :] = ws[yl * 2 + c]
 
-    pl.semaphore_wait(barrier, 6 + NI - 1)
+    pl.semaphore_wait(barrier, 5 + NI - 1)
+
+    def x_part(h, jj):
+        return xg.at[h, jj, pl.ds(0, PARTS[h] + GAIN_ROWS), :]
 
     def x_send(h, jj, dev):
-        send(xg.at[h, jj], xg.at[h, jj], xr.at[h, jj], dev)
+        send(f"x{h}", x_part(h, jj), x_part(h, jj), xr.at[h, jj], dev)
 
     def x_wait(h, jj):
-        arrived(xg.at[h, jj], xr.at[h, jj])
+        arrived(x_part(h, jj), xr.at[h, jj])
 
     def w_send(ii, half, dev):
-        send(wg.at[ii, half], wg.at[ii, half], wr.at[ii, half], dev)
+        send("w", wg.at[ii, half], wg.at[ii, half], wr.at[ii, half], dev)
 
     def w_wait(ii, half):
         arrived(wg.at[ii, half], wr.at[ii, half])
@@ -122,15 +121,13 @@
         x_send(h, j, dev_up)
         x_send(h, j, dev_down)
         x_send(h, j, dev_c)
-    send(wg.at[i, 0], wt.at[0], wtr.at[0], dev_yu)
-    send(wg.at[i, 1], wt.at[1], wtr.at[1], dev_yd)
     for half in range(2):
-        w_send(i, half, dev_xu)
-        w_send(i, half, dev_xd)
+        for dev in (dev_yh, dev_xu, dev_xd, dev_xf):
+            w_send(i, half, dev)
 
     mine_rows = pl.ds(pl.multiple_of(c * F, F), F)
     for dev, block in ((dev_c, yl * 2 + 1 - c), (dev_y, (1 - yl) * 2 + c), (dev_yc, (1 - yl) * 2 + 1 - c)):
-        send(ws.at[block], wo.at[i, yl, mine_rows, :], wor.at[i, yl, c], dev)
+        send("ws", ws.at[block], wo.at[i, yl, mine_rows, :], wor.at[i, yl, c], dev)
 
     def clear(r, carry):
         ext[:, pl.ds(8 + r * 128, 128), :] = jnp.zeros((3, 128, F), F32)
@@ -146,14 +143,10 @@
     x_send(1, jp, dev_c)
     x_wait(0, jp)
     x_send(0, jp, dev_c)
-    arrived(wt.at[0], wtr.at[0])
-    send(wt.at[0], wg.at[i_yd, 0], wr.at[i_yd, 0], dev_yu)
-    arrived(wt.at[1], wtr.at[1])
-    send(wt.at[1], wg.at[i_yu, 1], wr.at[i_yu, 1], dev_yd)
     for half in range(2):
         w_wait(pair, half)
-        w_send(pair, half, dev_xu)
-        w_send(pair, half, dev_xd)
+        for dev in (dev_xu, dev_xd, dev_xf):
+            w_send(pair, half, dev)
 
     def x_step(s):
         for plus in (True, False):
@@ -171,7 +164,11 @@
                     continue
                 x_wait(h, jj)
                 if name == "par1" and s == 3:
-                    send_if(c == (0 if plus else 1), xg.at[h, jj], xg.at[h, jj], xr.at[h, jj], dev)
+                    if plus:
+                        counts["x1"] += 1
+                    pl.when(c == (0 if plus else 1))(
+                        transfer("x1", x_part(h, jj), x_part(h, jj), xr.at[h, jj], dev).start
+                    )
                 elif s < hops[name]:
                     x_send(h, jj, dev)
                 if name == "own0":
@@ -200,16 +197,19 @@
         x_other_core(s)
 
         def body(k, carry):
-            zo, h, r = origin(s, k // 8), (k // 4) % 2, k % 4
-            rows = pl.ds(pl.multiple_of(r * 128, 128), 128)
+            zo, r = origin(s, k // 8), k % 8
+            h = (r * 128 + T - STARTS[1]) // T
+            rows = pl.ds(pl.multiple_of(r * 128 - h * STARTS[1], 128), 128)
+            gain_rows = pl.ds(pl.multiple_of(PARTS[0] + h * (PARTS[1] - PARTS[0]), 16), GAIN_ROWS)
+            to = pl.ds(pl.multiple_of(r * 128, 128), 128)
             squares = None
             for b in range(4):
                 jj = zo * 4 + b
                 block = xg[h, jj, rows, :].astype(F32)
-                gains = jnp.sum(xg[h, jj, pl.ds(H, 16), :].astype(F32), axis=0, keepdims=True)
-                xs[h, zo, rows, b * F:(b + 1) * F] = (block * gains).astype(BF16)
+                gains = jnp.sum(xg[h, jj, gain_rows, :].astype(F32), axis=0, keepdims=True)
+                xs[zo, to, b * F:(b + 1) * F] = (block * gains).astype(BF16)
                 squares = block * block if squares is None else squares + block * block
-            ssq[pl.ds(pl.multiple_of(h * H + r * 128, 128), 128), :] += squares
+            ssq[to, :] += squares
             return carry
 
         lax.fori_loop(0, 8 * n_origins(s), body, 0)
@@ -221,7 +221,9 @@
             right = jnp.concatenate(
                 [jnp.concatenate([wg[zo, half, q] for half in range(2)], axis=0) for q in range(3)], axis=1
             )
-            product = jnp.dot(xs[h, zo], right, preferred_element_type=F32)
+            product = jnp.dot(
+                xs[zo, pl.ds(pl.multiple_of(h * H, H), H), :], right, preferred_element_type=F32
+            )
             for q in range(3):
                 ext[q, into, :] += product[:, q * F:(q + 1) * F]
             return carry
@@ -229,59 +231,43 @@
         lax.fori_loop(0, 2 * n_origins(s), body, 0)
 
     def o_send(ii, half, dev):
-        send(wo.at[ii, half], wo.at[ii, half], wor.at[ii, half, 0], dev)
+        send("o", wo.at[ii, half], wo.at[ii, half], wor.at[ii, half, 0], dev)
 
     def o_wait(ii, half):
         arrived(wo.at[ii, half], wor.at[ii, half, 0])
 
-    pd, pu = (pair + NI - 2) % NI, (pair + 2) % NI
-    far, pfar = (i + 4) % NI, (pair + 4) % NI
-
-    def pass_on(wait, forward, below, above):
-        for half in (0, 1):
-            wait(below, half)
-            if half == 0:
-                forward(below, 0, dev_xu)
-            wait(above, half)
-            if half == 1:
-                forward(above, 1, dev_xd)
-
+    others = [(ii + k) % NI for ii in (i, pair) for k in (2, 6, 4)]
     x_step(1)
-    pass_on(w_wait, w_send, ix_down, ix_up)
     prepare(0)
     x_step(2)
     x_late(1)
-    pass_on(w_wait, w_send, pd, pu)
     prepare(1)
+    x_step(3)
+    x_late(2)
     for yy, cc in ((yl, 1 - c), (1 - yl, c), (1 - yl, 1 - c)):
         rows = pl.ds(pl.multiple_of(cc * F, F), F)
         arrived(wo.at[i, yy, rows, :], wor.at[i, yy, cc])
+    prepare(2)
+    for ii in others:
+        for half in range(2):
+            w_wait(ii, half)
     for half in range(2):
-        for dev in (dev_yh, dev_xu, dev_xd):
+        for dev in (dev_yh, dev_xu, dev_xd, dev_xf):
             o_send(i, half, dev)
-    x_step(3)
-    x_late(2)
-    prepare(2)
-    for half in range(2):
-        w_wait(far, half)
-    for half in range(2):
-        w_wait(pfar, half)
     multiply(0)
     multiply(1)
     x_step(4)
+    x_late(3)
     for half in range(2):
         o_wait(pair, half)
-        for dev in (dev_xu, dev_xd):
+        for dev in (dev_xu, dev_xd, dev_xf):
             o_send(pair, half, dev)
-    x_late(3)
     prepare(3)
     multiply(2)
     x_late(4)
-    pass_on(o_wait, o_send, ix_down, ix_up)
     multiply(3)
     prepare(4)
     multiply(4)
-    pass_on(o_wait, o_send, pd, pu)
 
     def normalise(r, carry):
         rows = pl.ds(pl.multiple_of(r * 128, 128), 128)
@@ -291,8 +277,10 @@
         ext[:, into, :] = (ext[:, into, :] * inverse[None]).astype(BF16).astype(F32)
         return carry
 
-    lax.fori_loop(0, T // 128, normalise, 0)
-    send_if(i < NI - 1, ext.at[:, pl.ds(T, 8)], ext.at[:, pl.ds(0, 8)], hr, ((i + 1) % NI, j))
+    normalise(T // 128 - 1, 0)
+    halo = transfer("halo", ext.at[:, pl.ds(T, 8)], ext.at[:, pl.ds(0, 8)], hr, ((i + 1) % NI, j))
+    pl.when(i < NI - 1)(halo.start)
+    lax.fori_loop(0, T // 128 - 1, normalise, 0)
 
     rate_t, resid_t = rate[...], resid[...]
     scale_t = jnp.sqrt(one_minus_exp_neg(2.0 * rate_t))
@@ -305,42 +293,50 @@
     lam = [wide(lam_t, n) for n in range(ORDER)]
     tap = lambda t, q: jnp.broadcast_to(filt[t, q:q + 1, :], (CH, F))
 
-    @pl.when(i == 0)
-    def _():
-        ext[:, 6:8, :] = tail[...].astype(F32)
-
-    @pl.when(i > 0)
-    def _():
-        arrived(ext.at[:, pl.ds(0, 8)], hr)
-
     def chunk_rows(start, q):
         return ext[q, pl.ds(start, CH, stride=CL), :]
 
     kt, vt = [tap(t, 1) for t in range(3)], [tap(t, 2) for t in range(3)]
-    U = 4
+
+    def mix(k0, k1, k2, v0, v1, v2):
+        keys = kt[0] * k0 + kt[1] * k1 + kt[2] * k2
+        values = vt[0] * v0 + vt[1] * v1 + vt[2] * v2
+        return (keys * values).astype(BF16).astype(F32)
+
+    U = 6
 
     def first(it, carry):
         k1, k2, v1, v2 = carry[:4]
         state = list(carry[4:])
         for u in range(U):
-            s = it * U + u
+            s = 2 + it * U + u
             k0, v0 = chunk_rows(8 + s, 1), chunk_rows(8 + s, 2)
-            keys = kt[0] * k0 + kt[1] * k1 + kt[2] * k2
-            values = vt[0] * v0 + vt[1] * v1 + vt[2] * v2
-            m = (keys * values).astype(BF16).astype(F32)
+            m = mix(k0, k1, k2, v0, v1, v2)
             mx[s] = m
             state = [lam[n] * state[n] + m for n in range(ORDER)]
             k1, k2, v1, v2 = k0, k1, v0, v1
         return (k1, k2, v1, v2, *state)
 
     zero = jnp.zeros((CH, F), F32)
-    carry = lax.fori_loop(
-        0, CL // U, first,
-        (chunk_rows(7, 1), chunk_rows(6, 1), chunk_rows(7, 2), chunk_rows(6, 2)) + (zero,) * ORDER,
-    )
+    state = lax.fori_loop(
+        0, (CL - 2) // U, first,
+        (chunk_rows(9, 1), chunk_rows(8, 1), chunk_rows(9, 2), chunk_rows(8, 2)) + (zero,) * ORDER,
+    )[4:]
+
+    @pl.when(i == 0)
+    def _():
+        ext[:, 6:8, :] = tail[...].astype(F32)
+
+    @pl.when(i > 0)
+    def _():
+        arrived(ext.at[:, pl.ds(0, 8)], hr)
+
+    heads = [mix(*(chunk_rows(8 + s - back, q) for q in (1, 2) for back in range(3))) for s in range(2)]
+    mx[0], mx[1] = heads
     row8 = lax.broadcasted_iota(jnp.int32, (CH, F), 0)
     for n in range(ORDER):
-        total, r = carry[4 + n], jnp.broadcast_to(rate_t[n:n + 1, :], (CH, F))
+        r = jnp.broadcast_to(rate_t[n:n + 1, :], (CH, F))
+        total = state[n] + jnp.exp(-r * float(CL - 2)) * (lam[n] * heads[0] + heads[1])
         for shift in (1, 2, 4):
             moved = jnp.where(row8 >= shift, pltpu.roll(total, shift, axis=0), 0.0)
             total = total + jnp.exp(-r * float(CL * shift)) * moved
@@ -348,7 +344,7 @@
         endb[n:n + 1, :] = total[CH - 1:CH, :]
     ends[i] = endb[...]
     for k in range(1, NI):
-        send(endb, ends.at[i], er.at[i], ((i + k) % NI, j))
+        send("ends", endb, ends.at[i], er.at[i], ((i + k) % NI, j))
     start_t = st_in[...] / scale_t
     whole = jnp.exp(-rate_t * float(T))
     for k in range(1, NI):
@@ -369,11 +365,13 @@
         before = jnp.where(row8 >= 1, pltpu.roll(ts[n], 1, axis=0), 0.0)
         entering.append(before + jnp.exp(-r * chunk_start) * jnp.broadcast_to(mine[n:n + 1, :], (CH, F)))
 
+    V = 4
+
     def second(it, carry):
         q1, q2 = carry[:2]
         state = list(carry[2:])
-        for u in range(U):
-            s = it * U + u
+        for u in range(V):
+            s = it * V + u
             q0 = chunk_rows(8 + s, 0)
             query = qt[0] * q0 + qt[1] * q1 + qt[2] * q2
             m = mx[s]
@@ -385,10 +383,10 @@
             q1, q2 = q0, q1
         return (q1, q2, *state)
 
-    lax.fori_loop(0, CL // U, second, (chunk_rows(7, 0), chunk_rows(6, 0), *entering))
+    lax.fori_loop(0, CL // V, second, (chunk_rows(7, 0), chunk_rows(6, 0), *entering))
 
     def g_send(h, yy, dev):
-        send(gk.at[h, yy * 2 + c], gk.at[h, yy * 2 + c], gr.at[h, yy * 2 + c], dev)
+        send("g", gk.at[h, yy * 2 + c], gk.at[h, yy * 2 + c], gr.at[h, yy * 2 + c], dev)
 
     def g_wait(h, slot):
         arrived(gk.at[h, slot], gr.at[h, slot])
@@ -397,9 +395,9 @@
         gk[h, yl * 2 + c] = gf[h * H:(h + 1) * H, :].astype(BF16)
         g_send(h, yl, dev_y)
         g_send(h, yl, dev_c)
-    for half in range(2):
-        o_wait(far, half)
-        o_wait(pfar, half)
+    for ii in others:
+        for half in range(2):
+            o_wait(ii, half)
     for h in range(2):
         g_wait(h, (1 - yl) * 2 + c)
         g_send(h, 1 - yl, dev_c)
@@ -424,8 +422,9 @@
         if s > 0:
             arrived(rb.at[d, h, s - 1], rr.at[d, h, s - 1])
             total = total + rb[d, h, s - 1].astype(F32)
-        sb[d, h, s] = total.astype(BF16)
-        send(sb.at[d, h, s], rb.at[d, h, s], rr.at[d, h, s], dev_up if d == 0 else dev_down)
+        n = d * 7 + h * steps[d, 0] + s
+        sb[n] = total.astype(BF16)
+        send("sum", sb.at[n], rb.at[d, h, s], rr.at[d, h, s], dev_up if d == 0 else dev_down)
 
     for h in range(2):
         g_wait(h, yl * 2 + 1 - c)
@@ -452,11 +451,18 @@
             total = total + rb[d, h, last].astype(F32)
         out[rows, :] = total.astype(BF16)
 
-    for copy, cond in sends:
-        if cond is None:
-            copy.wait_send()
-        else:
-            pl.when(cond)(lambda copy=copy: copy.wait_send())
+    for group, refs in (
+        ("x0", xg.at[0, pl.ds(0, counts["x0"]), pl.ds(0, PARTS[0] + GAIN_ROWS), :]),
+        ("x1", xg.at[1, pl.ds(0, counts["x1"]), pl.ds(0, PARTS[1] + GAIN_ROWS), :]),
+        ("w", wg.at[pl.ds(0, counts["w"] // 2)]),
+        ("o", wo.at[pl.ds(0, counts["o"] // 2)]),
+        ("ws", ws.at[pl.ds(0, counts["ws"])]),
+        ("ends", ends.at[pl.ds(0, counts["ends"])]),
+        ("g", gk.at[:, pl.ds(0, counts["g"] // 2)]),
+        ("sum", sb.at[pl.ds(0, counts["sum"])]),
+    ):
+        all_sent(group, refs)
+    pl.when(i < NI - 1)(halo.wait_send)
 
 
 def local(activations, norm_gain, w_in, tail_rows, short_filter, decay_rate, residue, skip_gain, state_in, w_out):
@@ -468,10 +474,9 @@
         in_specs=[vmem] * 10,
         out_specs=(vmem, vmem),
         scratch_shapes=[
-            pltpu.VMEM((2, NJ, HG, F), BF16),
-            pltpu.VMEM((2, NZ, H, 4 * F), BF16),
+            pltpu.VMEM((2, NJ, max(PARTS) + GAIN_ROWS, F), BF16),
+            pltpu.VMEM((NZ, T, 4 * F), BF16),
             pltpu.VMEM((NI, 2, 3, 256, F), BF16),
-            pltpu.VMEM((2, 3, 256, F), BF16),
             pltpu.VMEM((3, T + 8, F), F32),
             pltpu.VMEM((T, F), F32),
             pltpu.VMEM((CL, CH, F), F32),
@@ -483,12 +488,11 @@
             pltpu.VMEM((4, F, F), BF16),
             pltpu.VMEM((NI, 2, 2 * F, F), BF16),
             pltpu.VMEM((2, NZ, H, F), F32),
+            pltpu.VMEM((14, H, F), BF16),
             pltpu.VMEM((2, 2, 4, H, F), BF16),
-            pltpu.VMEM((2, 2, 4, H, F), BF16),
-            dma((N_SEND,)),
+            dma((len(GROUPS),)),
             dma((2, NJ)),
             dma((NI, 2)),
-            dma((2,)),
             dma,
             dma((NI,)),
             dma((NI, 2, 2)),

time: 109 us -> 107 us (0.982)
  Pallas kernels: 106 us -> 104 us
    pallas_call x1, Pallas kernels: 106 us -> 104 us  [local(): pl.pallas_call(block_kernel, out_shape=(jax.ShapeDtypeStruct((T, F), BF16...]
where the time goes in v3:
time: 107 us; the launch traced here: 106 us
  Pallas kernels  104 us (97%)
  local copies, waits for them, and re-layouts  2.28 us (2%)
    pallas_call x1, Pallas kernels, local(): pl.pallas_call(block_kernel, out_shape=(jax.ShapeDtypeStruct((T, F), BF16...  104 us
    unnamed x4, local copies, waits for them, and re-layouts  2.28 us

profile of v3, /device:TPU:1, one launch (start us, length us, event | category | flops | bytes accessed | tf_op | source)
XLA Modules:
  0.0 106.4 jit_solution(13507678038712935778)
XLA Ops:
  0.6 103.5 %shard_map.113 = (bf16[1024,128]{1,0:T(8,128)(2,1)}, f32[16,128]{1,0:T(8,128)}) custom-call(bf16[1024,128]{1,0:T(8,128)(2,1)} %act.1, f32[1,128]{1,0:T(1,128)} %bitcast.14, bf16[3,512,128]{2,1,0:T(8,128)(2,1)} %bitcast.8, bf16[3,2,128]{2,1,0:T(2,128)(2,1)} %bitcast.13, f32[3,3,128]{2,1,0:T(4,128)} %filt.1, f32[16,128]{1,0:T(8,128)} %bitcast.9, ...), custom_call_target="tpu_custom_call" | custom-call | tf_op jit(solution)/shard_map/pallas_call | solution.py:471
  104.2 0.0 copy-start
  104.2 1.7 %copy.14 = bf16[1024,128]{1,0:T(8,128)(2,1)} copy(bf16[1024,128]{1,0:T(8,128)(2,1)} %get-tuple-element.8) | data formatting | bytes 524288
  105.8 0.0 copy-done
  105.8 0.6 copy.15
Async XLA Ops:
  104.2 1.7 %copy-start = (f32[16,128]{1,0:T(8,128)S(1)}, f32[16,128]{1,0:T(8,128)}, u32[]{:S(2)}) copy-start(f32[16,128]{1,0:T(8,128)} %get-tuple-element.5) | copy-start | bytes 24580

commit v4 on v3

--- a/solution.py
+++ b/solution.py
@@ -12,11 +12,14 @@
 NZ, NX = 8, 4
 T, F, D, ORDER = 1024, 128, 4096, 16
 H = T // 2
-PARTS = (384, 640)
-STARTS = (0, 384)
+PARTS = (448, 576)
+STARTS = (0, 448)
 GAIN_ROWS = 16
 CH = 8
 CL = T // CH
+NP = 4
+PR = CL // NP
+PT = T // NP
 GROUPS = {name: n for n, name in enumerate(("x0", "x1", "w", "o", "ws", "halo", "ends", "g", "sum"))}
 PLUS_HOPS = {"own0": 4, "own1": 3, "par1": 4}
 MINUS_HOPS = {"own0": 3, "own1": 4, "par1": 4}
@@ -116,14 +119,16 @@
     def w_wait(ii, half):
         arrived(wg.at[ii, half], wr.at[ii, half])
 
+    x_send(1, j, dev_y)
     for h in range(2):
-        x_send(h, j, dev_y)
         x_send(h, j, dev_up)
         x_send(h, j, dev_down)
+    x_send(0, j, dev_y)
+    for half in range(2):
+        for dev in (dev_xu, dev_xd, dev_xf):
+            w_send(i, half, dev)
+    for h in range(2):
         x_send(h, j, dev_c)
-    for half in range(2):
-        for dev in (dev_yh, dev_xu, dev_xd, dev_xf):
-            w_send(i, half, dev)
 
     mine_rows = pl.ds(pl.multiple_of(c * F, F), F)
     for dev, block in ((dev_c, yl * 2 + 1 - c), (dev_y, (1 - yl) * 2 + c), (dev_yc, (1 - yl) * 2 + 1 - c)):
@@ -144,16 +149,14 @@
     x_wait(0, jp)
     x_send(0, jp, dev_c)
     for half in range(2):
-        w_wait(pair, half)
-        for dev in (dev_xu, dev_xd, dev_xf):
-            w_send(pair, half, dev)
+        w_send(i, half, dev_yh)
 
     def x_step(s):
-        for plus in (True, False):
-            zo = (z + NZ - s) % NZ if plus else (z + s) % NZ
-            hops = PLUS_HOPS if plus else MINUS_HOPS
-            dev = dev_up if plus else dev_down
-            for name, h, yy in (("own0", 0, yl), ("own1", 1, yl), ("par1", 1, 1 - yl)):
+        for name, h, yy in (("own0", 0, yl), ("own1", 1, yl), ("par1", 1, 1 - yl)):
+            for plus in (True, False):
+                zo = (z + NZ - s) % NZ if plus else (z + s) % NZ
+                hops = PLUS_HOPS if plus else MINUS_HOPS
+                dev = dev_up if plus else dev_down
                 if s > hops[name]:
                     continue
                 jj = at(zo, yy, c)
@@ -197,11 +200,11 @@
         x_other_core(s)
 
         def body(k, carry):
-            zo, r = origin(s, k // 8), k % 8
-            h = (r * 128 + T - STARTS[1]) // T
-            rows = pl.ds(pl.multiple_of(r * 128 - h * STARTS[1], 128), 128)
+            zo, r = origin(s, k // 16), k % 16
+            h = (r * 64 + T - STARTS[1]) // T
+            rows = pl.ds(pl.multiple_of(r * 64 - h * STARTS[1], 64), 64)
             gain_rows = pl.ds(pl.multiple_of(PARTS[0] + h * (PARTS[1] - PARTS[0]), 16), GAIN_ROWS)
-            to = pl.ds(pl.multiple_of(r * 128, 128), 128)
+            to = pl.ds(pl.multiple_of(r * 64, 64), 64)
             squares = None
             for b in range(4):
                 jj = zo * 4 + b
@@ -212,23 +215,28 @@
             ssq[to, :] += squares
             return carry
 
-        lax.fori_loop(0, 8 * n_origins(s), body, 0)
+        lax.fori_loop(0, 16 * n_origins(s), body, 0)
 
     def multiply(s):
-        def body(k, carry):
-            zo, h = origin(s, k // 2), k % 2
+        origins = [origin(s, k) for k in range(n_origins(s))]
+
+        def body(h, carry):
             into = pl.ds(pl.multiple_of(8 + h * H, 8), H)
+            rows = pl.ds(pl.multiple_of(h * H, H), H)
+            left = jnp.concatenate([xs[zo, rows, :] for zo in origins], axis=1)
             right = jnp.concatenate(
-                [jnp.concatenate([wg[zo, half, q] for half in range(2)], axis=0) for q in range(3)], axis=1
+                [
+                    jnp.concatenate([wg[zo, half, q] for zo in origins for half in range(2)], axis=0)
+                    for q in range(3)
+                ],
+                axis=1,
             )
-            product = jnp.dot(
-                xs[zo, pl.ds(pl.multiple_of(h * H, H), H), :], right, preferred_element_type=F32
-            )
+            product = jnp.dot(left, right, preferred_element_type=F32)
             for q in range(3):
                 ext[q, into, :] += product[:, q * F:(q + 1) * F]
             return carry
 
-        lax.fori_loop(0, 2 * n_origins(s), body, 0)
+        lax.fori_loop(0, 2, body, 0)
 
     def o_send(ii, half, dev):
         send("o", wo.at[ii, half], wo.at[ii, half], wor.at[ii, half, 0], dev)
@@ -238,6 +246,10 @@
 
     others = [(ii + k) % NI for ii in (i, pair) for k in (2, 6, 4)]
     x_step(1)
+    for half in range(2):
+        w_wait(pair, half)
+        for dev in (dev_xu, dev_xd, dev_xf):
+            w_send(pair, half, dev)
     prepare(0)
     x_step(2)
     x_late(1)
@@ -251,21 +263,17 @@
     for ii in others:
         for half in range(2):
             w_wait(ii, half)
+    multiply(0)
+    multiply(1)
+    multiply(2)
+    x_step(4)
+    x_late(3)
+    prepare(3)
     for half in range(2):
         for dev in (dev_yh, dev_xu, dev_xd, dev_xf):
             o_send(i, half, dev)
-    multiply(0)
-    multiply(1)
-    x_step(4)
-    x_late(3)
-    for half in range(2):
-        o_wait(pair, half)
-        for dev in (dev_xu, dev_xd, dev_xf):
-            o_send(pair, half, dev)
-    prepare(3)
-    multiply(2)
+    multiply(3)
     x_late(4)
-    multiply(3)
     prepare(4)
     multiply(4)
 
@@ -345,6 +353,10 @@
     ends[i] = endb[...]
     for k in range(1, NI):
         send("ends", endb, ends.at[i], er.at[i], ((i + k) % NI, j))
+    for half in range(2):
+        o_wait(pair, half)
+        for dev in (dev_xu, dev_xd, dev_xf):
+            o_send(pair, half, dev)
     start_t = st_in[...] / scale_t
     whole = jnp.exp(-rate_t * float(T))
     for k in range(1, NI):
@@ -383,73 +395,76 @@
             q1, q2 = q0, q1
         return (q1, q2, *state)
 
-    lax.fori_loop(0, CL // V, second, (chunk_rows(7, 0), chunk_rows(6, 0), *entering))
-
-    def g_send(h, yy, dev):
-        send("g", gk.at[h, yy * 2 + c], gk.at[h, yy * 2 + c], gr.at[h, yy * 2 + c], dev)
-
-    def g_wait(h, slot):
-        arrived(gk.at[h, slot], gr.at[h, slot])
-
-    for h in range(2):
-        gk[h, yl * 2 + c] = gf[h * H:(h + 1) * H, :].astype(BF16)
-        g_send(h, yl, dev_y)
-        g_send(h, yl, dev_c)
-    for ii in others:
-        for half in range(2):
-            o_wait(ii, half)
-    for h in range(2):
-        g_wait(h, (1 - yl) * 2 + c)
-        g_send(h, 1 - yl, dev_c)
-
-    def partial(h, first_to, second_to):
-        left = jnp.concatenate([gk[h, slot] for slot in range(4)], axis=1)
+    def g_send(p, yy, dev):
+        send("g", gk.at[p, yy * 2 + c], gk.at[p, yy * 2 + c], gr.at[p, yy * 2 + c], dev)
+
+    def g_wait(p, slot):
+        arrived(gk.at[p, slot], gr.at[p, slot])
+
+    carry = (chunk_rows(7, 0), chunk_rows(6, 0), *entering)
+    for p in range(NP):
+        carry = lax.fori_loop(p * PR // V, (p + 1) * PR // V, second, carry)
+        for k in range(CH):
+            start = k * CL + p * PR
+            gk[p, yl * 2 + c, k * PR:(k + 1) * PR, :] = gf[start:start + PR, :].astype(BF16)
+        g_send(p, yl, dev_y)
+        g_send(p, yl, dev_c)
+    for p in range(NP):
+        g_wait(p, (1 - yl) * 2 + c)
+        g_send(p, 1 - yl, dev_c)
+        if p == 0:
+            for ii in others:
+                for half in range(2):
+                    o_wait(ii, half)
+
+    def partial(p, first_to, second_to):
+        left = jnp.concatenate([gk[p, slot] for slot in range(4)], axis=1)
         right = jnp.concatenate(
             [jnp.concatenate([wo[to, half] for half in range(2)], axis=0) for to in (first_to, second_to)], axis=1
         )
         product = jnp.dot(left, right, preferred_element_type=F32)
-        pa[h, first_to] = product[:, 0:F]
-        pa[h, second_to] = product[:, F:2 * F]
-
-    steps = {(d, h): 4 if d == h else 3 for d in range(2) for h in range(2)}
-
-    def target(d, h, s):
-        n = steps[d, h]
+        pa[p, first_to] = product[:, 0:F]
+        pa[p, second_to] = product[:, F:2 * F]
+
+    steps = {(d, p): 4 if d == p % 2 else 3 for d in range(2) for p in range(NP)}
+
+    def target(d, p, s):
+        n = steps[d, p]
         return (z + n - s) % NZ if d == 0 else (z + NZ - n + s) % NZ
 
-    def pass_sum(d, h, s):
-        total = pa[h, target(d, h, s)]
+    def pass_sum(d, p, s):
+        total = pa[p, target(d, p, s)]
         if s > 0:
-            arrived(rb.at[d, h, s - 1], rr.at[d, h, s - 1])
-            total = total + rb[d, h, s - 1].astype(F32)
-        n = d * 7 + h * steps[d, 0] + s
+            arrived(rb.at[d, p, s - 1], rr.at[d, p, s - 1])
+            total = total + rb[d, p, s - 1].astype(F32)
+        n = counts["sum"]
         sb[n] = total.astype(BF16)
-        send("sum", sb.at[n], rb.at[d, h, s], rr.at[d, h, s], dev_up if d == 0 else dev_down)
-
-    for h in range(2):
-        g_wait(h, yl * 2 + 1 - c)
-        g_wait(h, (1 - yl) * 2 + 1 - c)
-        partial(h, target(0, h, 0), target(1, h, 0))
-        pass_sum(0, h, 0)
-        pass_sum(1, h, 0)
-    for h in range(2):
-        partial(h, target(0, h, 1), target(1, h, 1))
-    for h in range(2):
-        partial(h, target(0, h, 2), target(1, h, 2))
-        partial(h, target(h, h, 3), z)
+        send("sum", sb.at[n], rb.at[d, p, s], rr.at[d, p, s], dev_up if d == 0 else dev_down)
+
+    for p in range(NP):
+        g_wait(p, yl * 2 + 1 - c)
+        g_wait(p, (1 - yl) * 2 + 1 - c)
+        partial(p, target(0, p, 0), target(1, p, 0))
+        pass_sum(0, p, 0)
+        pass_sum(1, p, 0)
     for s in range(1, 4):
-        for h in range(2):
+        for p in range(NP):
+            if s < 3:
+                partial(p, target(0, p, s), target(1, p, s))
+            else:
+                partial(p, target(p % 2, p, 3), z)
             for d in range(2):
-                if s < steps[d, h]:
-                    pass_sum(d, h, s)
-    for h in range(2):
-        rows = slice(h * H, (h + 1) * H)
-        total = pa[h, z] + act[rows, :].astype(F32)
+                if s < steps[d, p]:
+                    pass_sum(d, p, s)
+    for p in range(NP):
+        total = pa[p, z]
         for d in range(2):
-            last = steps[d, h] - 1
-            arrived(rb.at[d, h, last], rr.at[d, h, last])
-            total = total + rb[d, h, last].astype(F32)
-        out[rows, :] = total.astype(BF16)
+            last = steps[d, p] - 1
+            arrived(rb.at[d, p, last], rr.at[d, p, last])
+            total = total + rb[d, p, last].astype(F32)
+        for k in range(CH):
+            rows = slice(k * CL + p * PR, k * CL + (p + 1) * PR)
+            out[rows, :] = (total[k * PR:(k + 1) * PR, :] + act[rows, :].astype(F32)).astype(BF16)
 
     for group, refs in (
         ("x0", xg.at[0, pl.ds(0, counts["x0"]), pl.ds(0, PARTS[0] + GAIN_ROWS), :]),
@@ -458,7 +473,7 @@
         ("o", wo.at[pl.ds(0, counts["o"] // 2)]),
         ("ws", ws.at[pl.ds(0, counts["ws"])]),
         ("ends", ends.at[pl.ds(0, counts["ends"])]),
-        ("g", gk.at[:, pl.ds(0, counts["g"] // 2)]),
+        ("g", gk.at[:, pl.ds(0, counts["g"] // NP)]),
         ("sum", sb.at[pl.ds(0, counts["sum"])]),
     ):
         all_sent(group, refs)
@@ -484,20 +499,20 @@
             pltpu.VMEM((ORDER, F), F32),
             pltpu.VMEM((NI, ORDER, F), F32),
             pltpu.VMEM((T, F), F32),
-            pltpu.VMEM((2, 4, H, F), BF16),
+            pltpu.VMEM((NP, 4, PT, F), BF16),
             pltpu.VMEM((4, F, F), BF16),
             pltpu.VMEM((NI, 2, 2 * F, F), BF16),
-            pltpu.VMEM((2, NZ, H, F), F32),
-            pltpu.VMEM((14, H, F), BF16),
-            pltpu.VMEM((2, 2, 4, H, F), BF16),
+            pltpu.VMEM((NP, NZ, PT, F), F32),
+            pltpu.VMEM((7 * NP, PT, F), BF16),
+            pltpu.VMEM((2, NP, 4, PT, F), BF16),
             dma((len(GROUPS),)),
             dma((2, NJ)),
             dma((NI, 2)),
             dma,
             dma((NI,)),
             dma((NI, 2, 2)),
-            dma((2, 4)),
-            dma((2, 2, 4)),
+            dma((NP, 4)),
+            dma((2, NP, 4)),
         ],
         compiler_params=pltpu.CompilerParams(
             collective_id=0, has_side_effects=True, vmem_limit_bytes=56 << 20

time: 107 us -> 100 us (0.935)
  Pallas kernels: 104 us -> 96.3 us
    pallas_call x1, Pallas kernels: 104 us -> 96.3 us  [local(): pl.pallas_call(block_kernel, out_shape=(jax.ShapeDtypeStruct((T, F), BF16...]
where the time goes in v4:
time: 100 us; the launch traced here: 99.2 us
  Pallas kernels  96.3 us (96%)
  local copies, waits for them, and re-layouts  2.28 us (2%)
    pallas_call x1, Pallas kernels, local(): pl.pallas_call(block_kernel, out_shape=(jax.ShapeDtypeStruct((T, F), BF16...  96.3 us
    unnamed x4, local copies, waits for them, and re-layouts  2.28 us

profile of v4, /device:TPU:1, one launch (start us, length us, event | category | flops | bytes accessed | tf_op | source)
XLA Modules:
  0.0 99.2 jit_solution(16286245002097303510)
XLA Ops:
  0.6 96.3 %shard_map.113 = (bf16[1024,128]{1,0:T(8,128)(2,1)}, f32[16,128]{1,0:T(8,128)}) custom-call(bf16[1024,128]{1,0:T(8,128)(2,1)} %act.1, f32[1,128]{1,0:T(1,128)} %bitcast.14, bf16[3,512,128]{2,1,0:T(8,128)(2,1)} %bitcast.8, bf16[3,2,128]{2,1,0:T(2,128)(2,1)} %bitcast.13, f32[3,3,128]{2,1,0:T(4,128)} %filt.1, f32[16,128]{1,0:T(8,128)} %bitcast.9, ...), custom_call_target="tpu_custom_call" | custom-call | tf_op jit(solution)/shard_map/pallas_call | solution.py:486
  96.9 0.0 copy-start
  96.9 1.7 %copy.14 = bf16[1024,128]{1,0:T(8,128)(2,1)} copy(bf16[1024,128]{1,0:T(8,128)(2,1)} %get-tuple-element.8) | data formatting | bytes 524288
  98.6 0.0 copy-done
  98.6 0.6 copy.15
Async XLA Ops:
  96.9 1.7 %copy-start = (f32[16,128]{1,0:T(8,128)S(1)}, f32[16,128]{1,0:T(8,128)}, u32[]{:S(2)}) copy-start(f32[16,128]{1,0:T(8,128)} %get-tuple-element.5) | copy-start | bytes 24580

commit v5 on v4

--- a/solution.py
+++ b/solution.py
@@ -47,7 +47,6 @@
     ix_up, ix_down = (i + 2) % NI, (i + NI - 2) % NI
     pair = i + 1 - 2 * (i % 2)
     dev_xu, dev_xd, dev_yh = (ix_up, j), (ix_down, j), (pair, j)
-    dev_xf = ((i + 4) % NI, j)
     dev_yc = (i, at(z, 1 - yl, 1 - c))
 
     def transfer(group, src, dst, recv_sem, dev):
@@ -125,7 +124,7 @@
         x_send(h, j, dev_down)
     x_send(0, j, dev_y)
     for half in range(2):
-        for dev in (dev_xu, dev_xd, dev_xf):
+        for dev in (dev_xu, dev_xd):
             w_send(i, half, dev)
     for h in range(2):
         x_send(h, j, dev_c)
@@ -143,9 +142,9 @@
 
     jp = at(z, 1 - yl, c)
     x_wait(1, jp)
+    x_send(1, jp, dev_c)
     x_send(1, jp, dev_up)
     x_send(1, jp, dev_down)
-    x_send(1, jp, dev_c)
     x_wait(0, jp)
     x_send(0, jp, dev_c)
     for half in range(2):
@@ -166,6 +165,7 @@
                         x_send(h, jj, dev_c)
                     continue
                 x_wait(h, jj)
+                x_send(h, jj, dev_c)
                 if name == "par1" and s == 3:
                     if plus:
                         counts["x1"] += 1
@@ -176,7 +176,6 @@
                     x_send(h, jj, dev)
                 if name == "own0":
                     x_send(h, jj, dev_y)
-                x_send(h, jj, dev_c)
 
     def x_late(s):
         for zo in ((z + NZ - s) % NZ, (z + s) % NZ)[: 1 if s == NZ // 2 else 2]:
@@ -244,34 +243,55 @@
     def o_wait(ii, half):
         arrived(wo.at[ii, half], wor.at[ii, half, 0])
 
+    far, pfar = (i + 4) % NI, (pair + 4) % NI
     others = [(ii + k) % NI for ii in (i, pair) for k in (2, 6, 4)]
+
+    def pass_on(wait, forward, block):
+        below, above = (block + NI - 2) % NI, (block + 2) % NI
+        for half in (0, 1):
+            wait(below, half)
+            if half == 0:
+                forward(below, 0, dev_xu)
+            wait(above, half)
+            if half == 1:
+                forward(above, 1, dev_xd)
+
     x_step(1)
     for half in range(2):
         w_wait(pair, half)
-        for dev in (dev_xu, dev_xd, dev_xf):
+        for dev in (dev_xu, dev_xd):
             w_send(pair, half, dev)
+    pass_on(w_wait, w_send, i)
     prepare(0)
+    for yy, cc in ((yl, 1 - c), (1 - yl, c), (1 - yl, 1 - c)):
+        rows = pl.ds(pl.multiple_of(cc * F, F), F)
+        arrived(wo.at[i, yy, rows, :], wor.at[i, yy, cc])
+    for half in range(2):
+        o_send(i, half, dev_yh)
     x_step(2)
     x_late(1)
+    pass_on(w_wait, w_send, pair)
     prepare(1)
     x_step(3)
     x_late(2)
-    for yy, cc in ((yl, 1 - c), (1 - yl, c), (1 - yl, 1 - c)):
-        rows = pl.ds(pl.multiple_of(cc * F, F), F)
-        arrived(wo.at[i, yy, rows, :], wor.at[i, yy, cc])
     prepare(2)
-    for ii in others:
+    for ii in (far, pfar):
         for half in range(2):
             w_wait(ii, half)
+    for half in range(2):
+        for dev in (dev_xu, dev_xd):
+            o_send(i, half, dev)
+    for half in range(2):
+        o_wait(pair, half)
+        for dev in (dev_xu, dev_xd):
+            o_send(pair, half, dev)
     multiply(0)
     multiply(1)
     multiply(2)
     x_step(4)
     x_late(3)
     prepare(3)
-    for half in range(2):
-        for dev in (dev_yh, dev_xu, dev_xd, dev_xf):
-            o_send(i, half, dev)
+    pass_on(o_wait, o_send, i)
     multiply(3)
     x_late(4)
     prepare(4)
@@ -351,13 +371,10 @@
         ts[n] = total
         endb[n:n + 1, :] = total[CH - 1:CH, :]
     ends[i] = endb[...]
-    for k in range(1, NI):
+    for k in (3, 5, 4, 1, 7, 2, 6):
         send("ends", endb, ends.at[i], er.at[i], ((i + k) % NI, j))
-    for half in range(2):
-        o_wait(pair, half)
-        for dev in (dev_xu, dev_xd, dev_xf):
-            o_send(pair, half, dev)
     start_t = st_in[...] / scale_t
+    pass_on(o_wait, o_send, pair)
     whole = jnp.exp(-rate_t * float(T))
     for k in range(1, NI):
         arrived(ends.at[(i + k) % NI], er.at[(i + k) % NI])
@@ -413,7 +430,7 @@
         g_wait(p, (1 - yl) * 2 + c)
         g_send(p, 1 - yl, dev_c)
         if p == 0:
-            for ii in others:
+            for ii in (far, pfar):
                 for half in range(2):
                     o_wait(ii, half)
 

time: 100 us -> 97.7 us (0.977)
  Pallas kernels: 96.3 us -> 94.1 us
    pallas_call x1, Pallas kernels: 96.3 us -> 94.1 us  [local(): pl.pallas_call(block_kernel, out_shape=(jax.ShapeDtypeStruct((T, F), BF16...]
where the time goes in v5:
time: 97.7 us; the launch traced here: 97 us
  Pallas kernels  94.1 us (96%)
  local copies, waits for them, and re-layouts  2.28 us (2%)
    pallas_call x1, Pallas kernels, local(): pl.pallas_call(block_kernel, out_shape=(jax.ShapeDtypeStruct((T, F), BF16...  94.1 us
    unnamed x4, local copies, waits for them, and re-layouts  2.28 us

profile of v5, /device:TPU:1, one launch (start us, length us, event | category | flops | bytes accessed | tf_op | source)
XLA Modules:
  0.0 97.0 jit_solution(13861715975350889098)
XLA Ops:
  0.6 94.1 %shard_map.113 = (bf16[1024,128]{1,0:T(8,128)(2,1)}, f32[16,128]{1,0:T(8,128)}) custom-call(bf16[1024,128]{1,0:T(8,128)(2,1)} %act.1, f32[1,128]{1,0:T(1,128)} %bitcast.14, bf16[3,512,128]{2,1,0:T(8,128)(2,1)} %bitcast.8, bf16[3,2,128]{2,1,0:T(2,128)(2,1)} %bitcast.13, f32[3,3,128]{2,1,0:T(4,128)} %filt.1, f32[16,128]{1,0:T(8,128)} %bitcast.9, ...), custom_call_target="tpu_custom_call" | custom-call | tf_op jit(solution)/shard_map/pallas_call | solution.py:503
  94.7 0.0 copy-start
  94.8 1.7 %copy.14 = bf16[1024,128]{1,0:T(8,128)(2,1)} copy(bf16[1024,128]{1,0:T(8,128)(2,1)} %get-tuple-element.8) | data formatting | bytes 524288
  96.4 0.0 copy-done
  96.4 0.6 copy.15
Async XLA Ops:
  94.7 1.7 %copy-start = (f32[16,128]{1,0:T(8,128)S(1)}, f32[16,128]{1,0:T(8,128)}, u32[]{:S(2)}) copy-start(f32[16,128]{1,0:T(8,128)} %get-tuple-element.5) | copy-start | bytes 24580

commit v6 on v5

--- a/solution.py
+++ b/solution.py
@@ -36,7 +36,7 @@
     act, gain, w_local, tail, filt, rate, resid, skip, st_in, wout,
     out, st_out,
     xg, xs, wg, ext, ssq, mx, ts, endb, ends, gf, gk, ws, wo, pa, sb, rb,
-    ssem, xr, wr, hr, er, wor, gr, rr,
+    ssem, lr, xr, wr, hr, er, wor, gr, rr,
 ):
     i, j = lax.axis_index("ctx"), lax.axis_index("mp")
     z, yl, c = j // 4, (j // 2) % 2, j % 2
@@ -69,6 +69,20 @@
             src_ref=dst, dst_ref=dst, send_sem=ssem.at[0], recv_sem=recv_sem,
             device_id=dev_up, device_id_type=MESH,
         ).wait_recv()
+
+    own = [
+        pltpu.make_async_copy(
+            act.at[pl.ds(STARTS[h], PARTS[h]), :], xg.at[h, j, pl.ds(0, PARTS[h]), :], lr.at[h]
+        )
+        for h in range(2)
+    ]
+    own += [
+        pltpu.make_async_copy(w_local.at[:, pl.ds(half * 256, 256), :], wg.at[i, half], lr.at[2 + half])
+        for half in range(2)
+    ]
+    own += [pltpu.make_async_copy(wout.at[:, pl.ds(k * F, F)], ws.at[k], lr.at[4 + k]) for k in range(4)]
+    for copy in own:
+        copy.start()
 
     barrier = pltpu.get_barrier_semaphore()
 
@@ -93,15 +107,11 @@
                   jnp.where(row16 == 2, g_lo.astype(F32) + zero16, zero16)),
     ).astype(BF16)
     for h in range(2):
-        xg[h, j, 0:PARTS[h], :] = act[STARTS[h]:STARTS[h] + PARTS[h], :]
         xg[h, j, PARTS[h]:PARTS[h] + GAIN_ROWS, :] = g_rows
-    for half in range(2):
-        wg[i, half] = w_local[:, half * 256:(half + 1) * 256, :]
-    for k in range(4):
-        ws[k] = wout[:, k * F:(k + 1) * F]
+    pl.semaphore_wait(barrier, 5 + NI - 1)
+    for copy in own:
+        copy.wait()
     wo[i, yl, pl.ds(pl.multiple_of(c * F, F), F), :] = ws[yl * 2 + c]
-
-    pl.semaphore_wait(barrier, 5 + NI - 1)
 
     def x_part(h, jj):
         return xg.at[h, jj, pl.ds(0, PARTS[h] + GAIN_ROWS), :]
@@ -150,13 +160,13 @@
     for half in range(2):
         w_send(i, half, dev_yh)
 
-    def x_step(s):
+    def x_step(s, names=("own0", "own1", "par1")):
         for name, h, yy in (("own0", 0, yl), ("own1", 1, yl), ("par1", 1, 1 - yl)):
             for plus in (True, False):
                 zo = (z + NZ - s) % NZ if plus else (z + s) % NZ
                 hops = PLUS_HOPS if plus else MINUS_HOPS
                 dev = dev_up if plus else dev_down
-                if s > hops[name]:
+                if s > hops[name] or name not in names:
                     continue
                 jj = at(zo, yy, c)
                 if name == "par1" and s == 4:
@@ -286,14 +296,15 @@
         for dev in (dev_xu, dev_xd):
             o_send(pair, half, dev)
     multiply(0)
+    x_step(4, ("own0",))
     multiply(1)
+    x_step(4, ("own1", "par1"))
     multiply(2)
-    x_step(4)
     x_late(3)
     prepare(3)
     pass_on(o_wait, o_send, i)
+    x_late(4)
     multiply(3)
-    x_late(4)
     prepare(4)
     multiply(4)
 
@@ -480,8 +491,11 @@
             arrived(rb.at[d, p, last], rr.at[d, p, last])
             total = total + rb[d, p, last].astype(F32)
         for k in range(CH):
-            rows = slice(k * CL + p * PR, k * CL + (p + 1) * PR)
-            out[rows, :] = (total[k * PR:(k + 1) * PR, :] + act[rows, :].astype(F32)).astype(BF16)
+            start = k * CL + p * PR
+            rows = slice(start, start + PR)
+            h = int(start >= STARTS[1])
+            before = xg[h, j, start - STARTS[h]:start - STARTS[h] + PR, :]
+            out[rows, :] = (total[k * PR:(k + 1) * PR, :] + before.astype(F32)).astype(BF16)
 
     for group, refs in (
         ("x0", xg.at[0, pl.ds(0, counts["x0"]), pl.ds(0, PARTS[0] + GAIN_ROWS), :]),
@@ -498,12 +512,12 @@
 
 
 def local(activations, norm_gain, w_in, tail_rows, short_filter, decay_rate, residue, skip_gain, state_in, w_out):
-    vmem = pl.BlockSpec(memory_space=pltpu.VMEM)
+    vmem, anywhere = pl.BlockSpec(memory_space=pltpu.VMEM), pl.BlockSpec(memory_space=pl.ANY)
     dma = pltpu.SemaphoreType.DMA
     block_out, state_out = pl.pallas_call(
         block_kernel,
         out_shape=(jax.ShapeDtypeStruct((T, F), BF16), jax.ShapeDtypeStruct((ORDER, F), F32)),
-        in_specs=[vmem] * 10,
+        in_specs=[anywhere, vmem, anywhere, *[vmem] * 6, anywhere],
         out_specs=(vmem, vmem),
         scratch_shapes=[
             pltpu.VMEM((2, NJ, max(PARTS) + GAIN_ROWS, F), BF16),
@@ -523,6 +537,7 @@
             pltpu.VMEM((7 * NP, PT, F), BF16),
             pltpu.VMEM((2, NP, 4, PT, F), BF16),
             dma((len(GROUPS),)),
+            dma((8,)),
             dma((2, NJ)),
             dma((NI, 2)),
             dma,

time: 97.7 us -> 95.1 us (0.973)
  Pallas kernels: 94.1 us -> 91.7 us
    pallas_call x1, Pallas kernels: 94.1 us -> 91.7 us  [local(): pl.pallas_call(block_kernel, out_shape=(jax.ShapeDtypeStruct((T, F), BF16...]
where the time goes in v6:
time: 95.1 us; the launch traced here: 94.6 us
  Pallas kernels  91.7 us (96%)
  local copies, waits for them, and re-layouts  2.28 us (2%)
    pallas_call x1, Pallas kernels, local(): pl.pallas_call(block_kernel, out_shape=(jax.ShapeDtypeStruct((T, F), BF16...  91.7 us
    unnamed x4, local copies, waits for them, and re-layouts  2.28 us

profile of v6, /device:TPU:1, one launch (start us, length us, event | category | flops | bytes accessed | tf_op | source)
XLA Modules:
  0.0 94.6 jit_solution(329937638284398176)
XLA Ops:
  0.6 91.7 %shard_map.113 = (bf16[1024,128]{1,0:T(8,128)(2,1)}, f32[16,128]{1,0:T(8,128)}) custom-call(bf16[1024,128]{1,0:T(8,128)(2,1)} %act.1, f32[1,128]{1,0:T(1,128)} %bitcast.14, bf16[3,512,128]{2,1,0:T(8,128)(2,1)} %bitcast.8, bf16[3,2,128]{2,1,0:T(2,128)(2,1)} %bitcast.13, f32[3,3,128]{2,1,0:T(4,128)} %filt.1, f32[16,128]{1,0:T(8,128)} %bitcast.9, ...), custom_call_target="tpu_custom_call" | custom-call | tf_op jit(solution)/shard_map/pallas_call | solution.py:517
  92.3 0.0 copy-start
  92.3 1.7 %copy.14 = bf16[1024,128]{1,0:T(8,128)(2,1)} copy(bf16[1024,128]{1,0:T(8,128)(2,1)} %get-tuple-element.8) | data formatting | bytes 524288
  94.0 0.0 copy-done
  94.0 0.6 copy.15
Async XLA Ops:
  92.3 1.7 %copy-start = (f32[16,128]{1,0:T(8,128)S(1)}, f32[16,128]{1,0:T(8,128)}, u32[]{:S(2)}) copy-start(f32[16,128]{1,0:T(8,128)} %get-tuple-element.5) | copy-start | bytes 24580

commit v7 on v6

--- a/solution.py
+++ b/solution.py
@@ -296,14 +296,14 @@
         for dev in (dev_xu, dev_xd):
             o_send(pair, half, dev)
     multiply(0)
+    x_late(3)
     x_step(4, ("own0",))
     multiply(1)
     x_step(4, ("own1", "par1"))
     multiply(2)
-    x_late(3)
     prepare(3)
+    x_late(4)
     pass_on(o_wait, o_send, i)
-    x_late(4)
     multiply(3)
     prepare(4)
     multiply(4)

time: 95.1 us -> 94.5 us (level)
  no operation moved by 1% of the time
where the time goes in v7:
time: 94.5 us; the launch traced here: 94.1 us
  Pallas kernels  91.1 us (96%)
  local copies, waits for them, and re-layouts  2.28 us (2%)
    pallas_call x1, Pallas kernels, local(): pl.pallas_call(block_kernel, out_shape=(jax.ShapeDtypeStruct((T, F), BF16...  91.1 us
    unnamed x4, local copies, waits for them, and re-layouts  2.28 us

profile of v7, /device:TPU:1, one launch (start us, length us, event | category | flops | bytes accessed | tf_op | source)
XLA Modules:
  0.0 94.1 jit_solution(10462571095245151284)
XLA Ops:
  0.6 91.1 %shard_map.113 = (bf16[1024,128]{1,0:T(8,128)(2,1)}, f32[16,128]{1,0:T(8,128)}) custom-call(bf16[1024,128]{1,0:T(8,128)(2,1)} %act.1, f32[1,128]{1,0:T(1,128)} %bitcast.14, bf16[3,512,128]{2,1,0:T(8,128)(2,1)} %bitcast.8, bf16[3,2,128]{2,1,0:T(2,128)(2,1)} %bitcast.13, f32[3,3,128]{2,1,0:T(4,128)} %filt.1, f32[16,128]{1,0:T(8,128)} %bitcast.9, ...), custom_call_target="tpu_custom_call" | custom-call | tf_op jit(solution)/shard_map/pallas_call | solution.py:517
  91.8 0.0 copy-start
  91.8 1.7 %copy.14 = bf16[1024,128]{1,0:T(8,128)(2,1)} copy(bf16[1024,128]{1,0:T(8,128)(2,1)} %get-tuple-element.8) | data formatting | bytes 524288
  93.5 0.0 copy-done
  93.5 0.6 copy.15
Async XLA Ops:
  91.8 1.7 %copy-start = (f32[16,128]{1,0:T(8,128)S(1)}, f32[16,128]{1,0:T(8,128)}, u32[]{:S(2)}) copy-start(f32[16,128]{1,0:T(8,128)} %get-tuple-element.5) | copy-start | bytes 24580
